TPU v7x, 512 devices: a whole 4x4x16 slice. The times are simulated.
512 devices in a mesh: gx: 4 (over x), gy: 4 (over y), gz: 32 (over z, core).
Axes of the slice: x: 4, y: 4, z: 16, core: 2. Of those that a mesh axis runs over, the one named last changes fastest.
Arguments:
- displacement: bfloat16 [4, 4, 32, 768, 128], P('gx', 'gy', 'gz'), may hold values from -6 to 6
- flexibility: bfloat16 [4, 4, 32, 768, 768], P('gx', 'gy', 'gz'), as said below
- schur: bfloat16 [4, 4, 32, 768, 768], P('gx', 'gy', 'gz'), as said below
- face_rows: int32 [4, 4, 32, 768], P('gx', 'gy', 'gz'), may hold values from 0 to 767, as said below
- multiplicity: int32 [4, 4, 32, 768], P('gx', 'gy', 'gz'), may hold values from 2 to 8, as said below
Outputs:
- multipliers: float32 [4, 4, 32, 768, 128], P('gx', 'gy', 'gz')
Inputs may be any that keep to these rules, and one draw needn't show every extreme that they name: `flexibility`: symmetric and positive definite. `schur`: symmetric and positive definite. `face_rows`: an interface unknown may be constrained by several slots of its subdomain. `multiplicity`: each value is 2, 4 or 8; a slot and its partner slot carry the same value.
All inputs are finite; a program needn't handle non-finite values.
Results may differ from a plain program's by a relative error of at most 0.017.
Values may be sent and summed in bfloat16 or wider, within the bound.
No kernel may reach another device: no remote copies, remote signals or barrier semaphores. Data moves between devices by JAX's collectives and lax.ppermute only.
A program may use at most 64 MiB of HBM per device.

v0:
```python
import jax
import jax.numpy as jnp
from jax import lax
from jax.sharding import Mesh
from jax.sharding import PartitionSpec as P

ITERS = 3
GZ = ("gz_0", "gz_1")


def padded(value, sides, width):
    for axis, dim in sides:
        devices, length = (lax.axis_size(axis), value.shape[dim])
        up = [(i, (i + 1) % devices) for i in range(devices - 1)]
        down = [(j, i) for i, j in up]
        last = lax.slice_in_dim(value, length - width, length, axis=dim)
        initial = lax.slice_in_dim(value, 0, width, axis=dim)
        before = lax.ppermute(last, axis, up)
        after = lax.ppermute(initial, axis, down)
        value = jnp.concatenate([before, value, after], axis=dim)
    return value


def sent_to_all(value, axis):
    copies = jnp.broadcast_to(value, (lax.axis_size(axis), *value.shape))
    return lax.all_to_all(copies, axis, split_axis=0, concat_axis=0, tiled=True)


def over_copies(value, axis):
    everything = sent_to_all(value, axis)
    return jnp.sum(everything, axis=0)


def by_axis(value, axes):
    far, near = axes
    return over_copies(over_copies(value, near), far)


def in_one(arrays, axis):
    ravelled, at, done = (jnp.concatenate([a.reshape(-1) for a in arrays]), 0, [])
    so_far = by_axis(ravelled, axis)
    for a in arrays:
        done.append(so_far[at : at + a.size].reshape(a.shape))
        at += a.size
    return tuple(done)


def shards(displacement, flexibility, schur, face_rows, multiplicity):
    width = flexibility.shape[-1]
    loads = displacement.shape[-1]
    slots = face_rows.shape[-1]
    face_len = slots // 6
    displaced = displacement.reshape(width, loads)
    flex_op = flexibility.reshape(width, width)
    schur_op = schur.reshape(width, width)
    row_list = face_rows.reshape(slots)
    weight = 2.0 / multiplicity.reshape(slots, 1).astype(jnp.float32)
    index_x = lax.axis_index("gx")
    index_y = lax.axis_index("gy")
    index_z = lax.axis_index(GZ)
    have = jnp.stack(
        [
            index_x > 0,
            index_x < lax.axis_size("gx") - 1,
            index_y > 0,
            index_y < lax.axis_size("gy") - 1,
            index_z > 0,
            index_z < lax.axis_size(GZ) - 1,
        ]
    )
    inner = jnp.repeat(jnp.where(have, 0.5, 1.0).astype(jnp.float32), face_len).reshape(slots, 1)
    columns = jnp.arange(width, dtype=jnp.int32).reshape(1, width)
    pick_table = (row_list.reshape(slots, 1) == columns).astype(jnp.bfloat16)
    spread_table = (row_list.reshape(slots, 1) == columns).astype(jnp.float32).T

    def own_faces(values):
        return jnp.dot(pick_table, values, preferred_element_type=jnp.float32).reshape(
            6, face_len, loads
        )

    def jump(values):
        own = own_faces(values)
        own_half = own.astype(jnp.bfloat16)
        near_x = padded(own_half[0:2], (("gx", 0),), 1)
        near_y = padded(own_half[2:4], (("gy", 0),), 1)
        near_z = padded(own_half[4:6], ((GZ, 0),), 1)
        partner = jnp.stack([near_x[0], near_x[3], near_y[0], near_y[3], near_z[0], near_z[3]])
        return (own - partner.astype(jnp.float32)).reshape(slots, loads)

    def spread(values):
        return jnp.dot(
            spread_table,
            values,
            precision=lax.Precision.HIGHEST,
            preferred_element_type=jnp.float32,
        ).astype(jnp.bfloat16)

    def flex_apply(values):
        return jump(
            jnp.dot(flex_op, spread(values), preferred_element_type=jnp.float32).astype(
                jnp.bfloat16
            )
        )

    def precondition(values):
        return weight * jump(
            jnp.dot(schur_op, spread(weight * values), preferred_element_type=jnp.float32).astype(
                jnp.bfloat16
            )
        )

    def local_inner(left, right):
        return jnp.sum(inner * left * right, axis=0)

    residual = jump(displaced)
    solution = jnp.zeros((slots, loads), jnp.float32)

    def pair_totals(res_now, smooth_now, image_now):
        return in_one(
            (local_inner(res_now, smooth_now), local_inner(smooth_now, image_now)),
            (("gx", "gy"), ("gz_0", "gz_1")),
        )

    smoothed = precondition(residual)
    image_z = flex_apply(smoothed)
    rho_now, curvature = pair_totals(residual, smoothed, image_z)
    step_len = rho_now / curvature
    direction = smoothed
    along = image_z
    for iteration in range(ITERS):
        solution = solution + step_len * direction
        residual = residual - step_len * along
        if iteration + 1 < ITERS:
            smoothed = precondition(residual)
            image_z = flex_apply(smoothed)
            rho_next, curvature = pair_totals(residual, smoothed, image_z)
            ratio = rho_next / rho_now
            step_len = rho_next / (curvature - ratio * rho_next / step_len)
            direction = smoothed + ratio * direction
            along = image_z + ratio * along
            rho_now = rho_next
    return solution.reshape(1, 1, 1, slots, loads)


def solution(mesh):
    torus = Mesh(
        mesh.devices.reshape(mesh.shape["gx"], mesh.shape["gy"], 16, 2),
        ("gx", "gy", "gz_0", "gz_1"),
    )
    return jax.shard_map(
        shards,
        mesh=torus,
        in_specs=(
            P("gx", "gy", GZ, None, None),
            P("gx", "gy", GZ, None, None),
            P("gx", "gy", GZ, None, None),
            P("gx", "gy", GZ, None),
            P("gx", "gy", GZ, None),
        ),
        out_specs=P("gx", "gy", GZ, None, None),
        check_vma=False,
    )
```

profile of v0, /device:TPU:1, one launch (start us, length us, event | category | flops | bytes accessed | tf_op | source)
XLA Modules:
  0.0 264.8 jit_solution(453711152498923566)
XLA Ops:
  2.3 8.7 %collective-permute-start.5 = (bf16[1,128,128]{2,1,0:T(8,128)(2,1)S(1)}, bf16[1,128,128]{2,1,0:T(8,128)(2,1)S(1)}, u32[]{:S(2)}, u32[]{:S(2)}) collective-permute-start(bf16[1,128,128]{2,1,0:T(8,128)(2,1)S(1)} %get-tuple-element.52), channel_id=1, source_target_pairs={{1,0},{2,1},{3,2},{4,3},{5,4},{6,5},{7,6},{8,7},{9,8},{10,9},{11,1... | collective-permute-start | bytes 98312 | tf_op jit(solution)/shard_map/ppermute | solution.py:19
  14.3 4.0 %collective-permute-start.2 = (bf16[1,128,128]{2,1,0:T(8,128)(2,1)S(1)}, bf16[1,128,128]{2,1,0:T(8,128)(2,1)S(1)}, u32[]{:S(2)}, u32[]{:S(2)}) collective-permute-start(bf16[1,128,128]{2,1,0:T(8,128)(2,1)S(1)} %get-tuple-element.55), channel_id=1, source_target_pairs={{0,32},{32,64},{64,96},{1,33},{33,65},{65,97},{2,34},{34,66},{66,9... | collective-permute-start | bytes 98312 | tf_op jit(solution)/shard_map/ppermute | solution.py:18
  21.9 3.6 %collective-permute-done.1 = bf16[1,128,128]{2,1,0:T(8,128)(2,1)S(1)} collective-permute-done((bf16[1,128,128]{2,1,0:T(8,128)(2,1)S(1)}, bf16[1,128,128]{2,1,0:T(8,128)(2,1)S(1)}, u32[]{:S(2)}, u32[]{:S(2)}) %collective-permute-start.1) | collective-permute-done | bytes 32800 | tf_op jit(solution)/shard_map/ppermute | solution.py:19
  29.1 3.4 %collective-permute-start.6 = (bf16[1,128,128]{2,1,0:T(8,128)(2,1)S(1)}, bf16[1,128,128]{2,1,0:T(8,128)(2,1)S(1)}, u32[]{:S(2)}, u32[]{:S(2)}) collective-permute-start(bf16[1,128,128]{2,1,0:T(8,128)(2,1)S(1)} %get-tuple-element.51), channel_id=1, source_target_pairs={{0,128},{128,256},{256,384},{1,129},{129,257},{257,385},{2,130},{1... | collective-permute-start | bytes 98312 | tf_op jit(solution)/shard_map/ppermute | solution.py:18
  32.4 5.3 %collective-permute-start.11 = (bf16[1,128,128]{2,1,0:T(8,128)(2,1)S(1)}, bf16[1,128,128]{2,1,0:T(8,128)(2,1)S(1)}, u32[]{:S(2)}, u32[]{:S(2)}) collective-permute-start(bf16[1,128,128]{2,1,0:T(8,128)(2,1)S(1)} %get-tuple-element.46), channel_id=1, source_target_pairs={{1,0},{2,1},{3,2},{4,3},{5,4},{6,5},{7,6},{8,7},{9,8},{10,9},{11,1... | collective-permute-start | bytes 98312 | tf_op jit(solution)/shard_map/ppermute | solution.py:19
  40.9 4.0 %collective-permute-start.8 = (bf16[1,128,128]{2,1,0:T(8,128)(2,1)S(1)}, bf16[1,128,128]{2,1,0:T(8,128)(2,1)S(1)}, u32[]{:S(2)}, u32[]{:S(2)}) collective-permute-start(bf16[1,128,128]{2,1,0:T(8,128)(2,1)S(1)} %get-tuple-element.49), channel_id=1, source_target_pairs={{0,32},{32,64},{64,96},{1,33},{33,65},{65,97},{2,34},{34,66},{66,9... | collective-permute-start | bytes 98312 | tf_op jit(solution)/shard_map/ppermute | solution.py:18
  46.2 3.3 %collective-permute-done.7 = bf16[1,128,128]{2,1,0:T(8,128)(2,1)S(1)} collective-permute-done((bf16[1,128,128]{2,1,0:T(8,128)(2,1)S(1)}, bf16[1,128,128]{2,1,0:T(8,128)(2,1)S(1)}, u32[]{:S(2)}, u32[]{:S(2)}) %collective-permute-start.7) | collective-permute-done | bytes 32800 | tf_op jit(solution)/shard_map/ppermute | solution.py:19
  56.1 4.3 %collective-permute-start.17 = (bf16[1,128,128]{2,1,0:T(8,128)(2,1)S(1)}, bf16[1,128,128]{2,1,0:T(8,128)(2,1)S(1)}, u32[]{:S(2)}, u32[]{:S(2)}) collective-permute-start(bf16[1,128,128]{2,1,0:T(8,128)(2,1)S(1)} %get-tuple-element.40), channel_id=1, source_target_pairs={{1,0},{2,1},{3,2},{4,3},{5,4},{6,5},{7,6},{8,7},{9,8},{10,9},{11,1... | collective-permute-start | bytes 98312 | tf_op jit(solution)/shard_map/ppermute | solution.py:19
  64.1 4.0 %collective-permute-start.14 = (bf16[1,128,128]{2,1,0:T(8,128)(2,1)S(1)}, bf16[1,128,128]{2,1,0:T(8,128)(2,1)S(1)}, u32[]{:S(2)}, u32[]{:S(2)}) collective-permute-start(bf16[1,128,128]{2,1,0:T(8,128)(2,1)S(1)} %get-tuple-element.43), channel_id=1, source_target_pairs={{0,32},{32,64},{64,96},{1,33},{33,65},{65,97},{2,34},{34,66},{66,9... | collective-permute-start | bytes 98312 | tf_op jit(solution)/shard_map/ppermute | solution.py:18
  69.4 3.3 %collective-permute-done.13 = bf16[1,128,128]{2,1,0:T(8,128)(2,1)S(1)} collective-permute-done((bf16[1,128,128]{2,1,0:T(8,128)(2,1)S(1)}, bf16[1,128,128]{2,1,0:T(8,128)(2,1)S(1)}, u32[]{:S(2)}, u32[]{:S(2)}) %collective-permute-start.13) | collective-permute-done | bytes 32800 | tf_op jit(solution)/shard_map/ppermute | solution.py:19
  73.1 27.1 %all_to_all.36 = f32[32,1,256]{2,1,0:T(1,128)S(1)} all-to-all(f32[32,1,256]{2,1,0:T(1,128)S(1)} %broadcast_in_dim.40), channel_id=1, replica_groups=mesh['gx'=4,'gy'=4,'gz_0'=16,'gz_1'=2] {'gz_0','gz_1'}, dimensions={0} | all-to-all | bytes 65536 | tf_op jit(solution)/shard_map/all_to_all | solution.py:26
  100.3 10.5 %all_to_all.37 = f32[16,1,256]{2,1,0:T(1,128)S(1)} all-to-all(f32[16,1,256]{2,1,0:T(1,128)S(1)} %broadcast_in_dim.41), channel_id=1, replica_groups=mesh['gx'=4,'gy'=4,'gz_0'=16,'gz_1'=2] {'gx','gy'}, dimensions={0} | all-to-all | bytes 32768 | tf_op jit(solution)/shard_map/all_to_all | solution.py:26
  117.0 4.8 %collective-permute-start.23 = (bf16[1,128,128]{2,1,0:T(8,128)(2,1)S(1)}, bf16[1,128,128]{2,1,0:T(8,128)(2,1)S(1)}, u32[]{:S(2)}, u32[]{:S(2)}) collective-permute-start(bf16[1,128,128]{2,1,0:T(8,128)(2,1)S(1)} %get-tuple-element.34), channel_id=1, source_target_pairs={{1,0},{2,1},{3,2},{4,3},{5,4},{6,5},{7,6},{8,7},{9,8},{10,9},{11,1... | collective-permute-start | bytes 98312 | tf_op jit(solution)/shard_map/ppermute | solution.py:19
  125.1 4.0 %collective-permute-start.20 = (bf16[1,128,128]{2,1,0:T(8,128)(2,1)S(1)}, bf16[1,128,128]{2,1,0:T(8,128)(2,1)S(1)}, u32[]{:S(2)}, u32[]{:S(2)}) collective-permute-start(bf16[1,128,128]{2,1,0:T(8,128)(2,1)S(1)} %get-tuple-element.37), channel_id=1, source_target_pairs={{0,32},{32,64},{64,96},{1,33},{33,65},{65,97},{2,34},{34,66},{66,9... | collective-permute-start | bytes 98312 | tf_op jit(solution)/shard_map/ppermute | solution.py:18
  130.5 3.3 %collective-permute-done.19 = bf16[1,128,128]{2,1,0:T(8,128)(2,1)S(1)} collective-permute-done((bf16[1,128,128]{2,1,0:T(8,128)(2,1)S(1)}, bf16[1,128,128]{2,1,0:T(8,128)(2,1)S(1)}, u32[]{:S(2)}, u32[]{:S(2)}) %collective-permute-start.19) | collective-permute-done | bytes 32800 | tf_op jit(solution)/shard_map/ppermute | solution.py:19
  134.1 2.8 %fusion.61 = bf16[768,128]{1,0:T(8,128)(2,1)} fusion(f32[768,128]{1,0:T(8,128)S(1)} %fusion.79, s32[768]{0:T(1024)S(1)} %reduce.6), kind=kOutput, calls=%fused_computation.50 | convolution fusion | flops 906657792 | bytes 592896 | tf_op jit(solution)/shard_map/dot_general | solution.py:91
  136.9 2.4 fusion.99
  141.6 4.2 %collective-permute-start.29 = (bf16[1,128,128]{2,1,0:T(8,128)(2,1)S(1)}, bf16[1,128,128]{2,1,0:T(8,128)(2,1)S(1)}, u32[]{:S(2)}, u32[]{:S(2)}) collective-permute-start(bf16[1,128,128]{2,1,0:T(8,128)(2,1)S(1)} %get-tuple-element.28), channel_id=1, source_target_pairs={{1,0},{2,1},{3,2},{4,3},{5,4},{6,5},{7,6},{8,7},{9,8},{10,9},{11,1... | collective-permute-start | bytes 98312 | tf_op jit(solution)/shard_map/ppermute | solution.py:19
  149.2 4.0 %collective-permute-start.26 = (bf16[1,128,128]{2,1,0:T(8,128)(2,1)S(1)}, bf16[1,128,128]{2,1,0:T(8,128)(2,1)S(1)}, u32[]{:S(2)}, u32[]{:S(2)}) collective-permute-start(bf16[1,128,128]{2,1,0:T(8,128)(2,1)S(1)} %get-tuple-element.31), channel_id=1, source_target_pairs={{0,32},{32,64},{64,96},{1,33},{33,65},{65,97},{2,34},{34,66},{66,9... | collective-permute-start | bytes 98312 | tf_op jit(solution)/shard_map/ppermute | solution.py:18
  154.5 3.3 %collective-permute-done.25 = bf16[1,128,128]{2,1,0:T(8,128)(2,1)S(1)} collective-permute-done((bf16[1,128,128]{2,1,0:T(8,128)(2,1)S(1)}, bf16[1,128,128]{2,1,0:T(8,128)(2,1)S(1)}, u32[]{:S(2)}, u32[]{:S(2)}) %collective-permute-start.25) | collective-permute-done | bytes 32800 | tf_op jit(solution)/shard_map/ppermute | solution.py:19
  158.2 17.6 %all_to_all.38 = f32[32,1,256]{2,1,0:T(1,128)} all-to-all(f32[32,1,256]{2,1,0:T(1,128)S(1)} %broadcast_in_dim.42), channel_id=1, replica_groups=mesh['gx'=4,'gy'=4,'gz_0'=16,'gz_1'=2] {'gz_0','gz_1'}, dimensions={0} | all-to-all | bytes 65536 | tf_op jit(solution)/shard_map/all_to_all | solution.py:26
  176.6 9.7 %all_to_all.39 = f32[16,1,256]{2,1,0:T(1,128)} all-to-all(f32[16,1,256]{2,1,0:T(1,128)S(1)} %broadcast_in_dim.43), channel_id=1, replica_groups=mesh['gx'=4,'gy'=4,'gz_0'=16,'gz_1'=2] {'gx','gy'}, dimensions={0} | all-to-all | bytes 32768 | tf_op jit(solution)/shard_map/all_to_all | solution.py:26
  189.5 3.0 %fusion.62 = bf16[768,128]{1,0:T(8,128)(2,1)S(1)} fusion(s32[768]{0:T(1024)} %copy-done.5, f32[768,128]{1,0:T(8,128)S(1)} %multiply_subtract_fusion, f32[768]{0:T(1024)S(1)} %divide_reduce_fusion), kind=kOutput, calls=%fused_computation.51 | convolution fusion | flops 906756096 | bytes 595968 | tf_op jit(solution)/shard_map/dot_general | solution.py:91
  195.7 4.5 %collective-permute-start.35 = (bf16[1,128,128]{2,1,0:T(8,128)(2,1)S(1)}, bf16[1,128,128]{2,1,0:T(8,128)(2,1)S(1)}, u32[]{:S(2)}, u32[]{:S(2)}) collective-permute-start(bf16[1,128,128]{2,1,0:T(8,128)(2,1)S(1)} %get-tuple-element.22), channel_id=1, source_target_pairs={{1,0},{2,1},{3,2},{4,3},{5,4},{6,5},{7,6},{8,7},{9,8},{10,9},{11,1... | collective-permute-start | bytes 98312 | tf_op jit(solution)/shard_map/ppermute | solution.py:19
  203.7 4.0 %collective-permute-start.32 = (bf16[1,128,128]{2,1,0:T(8,128)(2,1)S(1)}, bf16[1,128,128]{2,1,0:T(8,128)(2,1)S(1)}, u32[]{:S(2)}, u32[]{:S(2)}) collective-permute-start(bf16[1,128,128]{2,1,0:T(8,128)(2,1)S(1)} %get-tuple-element.25), channel_id=1, source_target_pairs={{0,32},{32,64},{64,96},{1,33},{33,65},{65,97},{2,34},{34,66},{66,9... | collective-permute-start | bytes 98312 | tf_op jit(solution)/shard_map/ppermute | solution.py:18
  209.3 3.1 %collective-permute-done.31 = bf16[1,128,128]{2,1,0:T(8,128)(2,1)S(1)} collective-permute-done((bf16[1,128,128]{2,1,0:T(8,128)(2,1)S(1)}, bf16[1,128,128]{2,1,0:T(8,128)(2,1)S(1)}, u32[]{:S(2)}, u32[]{:S(2)}) %collective-permute-start.31) | collective-permute-done | bytes 32800 | tf_op jit(solution)/shard_map/ppermute | solution.py:19
  212.7 2.8 %fusion.63 = bf16[768,128]{1,0:T(8,128)(2,1)} fusion(f32[768,128]{1,0:T(8,128)S(1)} %fusion.78, s32[768]{0:T(1024)S(1)} %copy-done.6), kind=kOutput, calls=%fused_computation.52 | convolution fusion | flops 906657792 | bytes 592896 | tf_op jit(solution)/shard_map/dot_general | solution.py:91
  220.2 4.2 %collective-permute-start.41 = (bf16[1,128,128]{2,1,0:T(8,128)(2,1)S(1)}, bf16[1,128,128]{2,1,0:T(8,128)(2,1)S(1)}, u32[]{:S(2)}, u32[]{:S(2)}) collective-permute-start(bf16[1,128,128]{2,1,0:T(8,128)(2,1)S(1)} %get-tuple-element.16), channel_id=1, source_target_pairs={{1,0},{2,1},{3,2},{4,3},{5,4},{6,5},{7,6},{8,7},{9,8},{10,9},{11,1... | collective-permute-start | bytes 98312 | tf_op jit(solution)/shard_map/ppermute | solution.py:19
  227.8 4.0 %collective-permute-start.38 = (bf16[1,128,128]{2,1,0:T(8,128)(2,1)S(1)}, bf16[1,128,128]{2,1,0:T(8,128)(2,1)S(1)}, u32[]{:S(2)}, u32[]{:S(2)}) collective-permute-start(bf16[1,128,128]{2,1,0:T(8,128)(2,1)S(1)} %get-tuple-element.19), channel_id=1, source_target_pairs={{0,32},{32,64},{64,96},{1,33},{33,65},{65,97},{2,34},{34,66},{66,9... | collective-permute-start | bytes 98312 | tf_op jit(solution)/shard_map/ppermute | solution.py:18
  233.1 3.3 %collective-permute-done.37 = bf16[1,128,128]{2,1,0:T(8,128)(2,1)S(1)} collective-permute-done((bf16[1,128,128]{2,1,0:T(8,128)(2,1)S(1)}, bf16[1,128,128]{2,1,0:T(8,128)(2,1)S(1)}, u32[]{:S(2)}, u32[]{:S(2)}) %collective-permute-start.37) | collective-permute-done | bytes 32800 | tf_op jit(solution)/shard_map/ppermute | solution.py:19
  236.8 17.2 %all_to_all.40 = f32[32,1,256]{2,1,0:T(1,128)S(1)} all-to-all(f32[32,1,256]{2,1,0:T(1,128)S(1)} %broadcast_in_dim.44), channel_id=1, replica_groups=mesh['gx'=4,'gy'=4,'gz_0'=16,'gz_1'=2] {'gz_0','gz_1'}, dimensions={0} | all-to-all | bytes 65536 | tf_op jit(solution)/shard_map/all_to_all | solution.py:26
  254.1 9.7 %all_to_all.41 = f32[16,1,256]{2,1,0:T(1,128)S(1)} all-to-all(f32[16,1,256]{2,1,0:T(1,128)S(1)} %broadcast_in_dim.45), channel_id=1, replica_groups=mesh['gx'=4,'gy'=4,'gz_0'=16,'gz_1'=2] {'gx','gy'}, dimensions={0} | all-to-all | bytes 32768 | tf_op jit(solution)/shard_map/all_to_all | solution.py:26
  (178 shorter events, 70.1 us)
Async XLA Ops:
  2.3 23.3 %collective-permute-start.5 = (bf16[1,128,128]{2,1,0:T(8,128)(2,1)S(1)}, bf16[1,128,128]{2,1,0:T(8,128)(2,1)S(1)}, u32[]{:S(2)}, u32[]{:S(2)}) collective-permute-start(bf16[1,128,128]{2,1,0:T(8,128)(2,1)S(1)} %get-tuple-element.52), channel_id=1, source_target_pairs={{1,0},{2,1},{3,2},{4,3},{5,4},{6,5},{7,6},{8,7},{9,8},{10,9},{11,1... | collective-permute-start | bytes 98312 | tf_op jit(solution)/shard_map/ppermute | solution.py:19
  11.1 14.5 %collective-permute-start.4 = (bf16[1,128,128]{2,1,0:T(8,128)(2,1)S(1)}, bf16[1,128,128]{2,1,0:T(8,128)(2,1)S(1)}, u32[]{:S(2)}, u32[]{:S(2)}) collective-permute-start(bf16[1,128,128]{2,1,0:T(8,128)(2,1)S(1)} %get-tuple-element.53), channel_id=1, source_target_pairs={{0,1},{1,2},{2,3},{3,4},{4,5},{5,6},{6,7},{7,8},{8,9},{9,10},{10,1... | collective-permute-start | bytes 98312 | tf_op jit(solution)/shard_map/ppermute | solution.py:18
  13.0 12.6 %collective-permute-start.3 = (bf16[1,128,128]{2,1,0:T(8,128)(2,1)S(1)}, bf16[1,128,128]{2,1,0:T(8,128)(2,1)S(1)}, u32[]{:S(2)}, u32[]{:S(2)}) collective-permute-start(bf16[1,128,128]{2,1,0:T(8,128)(2,1)S(1)} %get-tuple-element.54), channel_id=1, source_target_pairs={{32,0},{64,32},{96,64},{33,1},{65,33},{97,65},{34,2},{66,34},{98,6... | collective-permute-start | bytes 98312 | tf_op jit(solution)/shard_map/ppermute | solution.py:19
  14.3 11.2 %collective-permute-start.2 = (bf16[1,128,128]{2,1,0:T(8,128)(2,1)S(1)}, bf16[1,128,128]{2,1,0:T(8,128)(2,1)S(1)}, u32[]{:S(2)}, u32[]{:S(2)}) collective-permute-start(bf16[1,128,128]{2,1,0:T(8,128)(2,1)S(1)} %get-tuple-element.55), channel_id=1, source_target_pairs={{0,32},{32,64},{64,96},{1,33},{33,65},{65,97},{2,34},{34,66},{66,9... | collective-permute-start | bytes 98312 | tf_op jit(solution)/shard_map/ppermute | solution.py:18
  29.1 15.9 %collective-permute-start.6 = (bf16[1,128,128]{2,1,0:T(8,128)(2,1)S(1)}, bf16[1,128,128]{2,1,0:T(8,128)(2,1)S(1)}, u32[]{:S(2)}, u32[]{:S(2)}) collective-permute-start(bf16[1,128,128]{2,1,0:T(8,128)(2,1)S(1)} %get-tuple-element.51), channel_id=1, source_target_pairs={{0,128},{128,256},{256,384},{1,129},{129,257},{257,385},{2,130},{1... | collective-permute-start | bytes 98312 | tf_op jit(solution)/shard_map/ppermute | solution.py:18
  32.4 17.2 %collective-permute-start.11 = (bf16[1,128,128]{2,1,0:T(8,128)(2,1)S(1)}, bf16[1,128,128]{2,1,0:T(8,128)(2,1)S(1)}, u32[]{:S(2)}, u32[]{:S(2)}) collective-permute-start(bf16[1,128,128]{2,1,0:T(8,128)(2,1)S(1)} %get-tuple-element.46), channel_id=1, source_target_pairs={{1,0},{2,1},{3,2},{4,3},{5,4},{6,5},{7,6},{8,7},{9,8},{10,9},{11,1... | collective-permute-start | bytes 98312 | tf_op jit(solution)/shard_map/ppermute | solution.py:19
  37.7 12.0 %collective-permute-start.10 = (bf16[1,128,128]{2,1,0:T(8,128)(2,1)S(1)}, bf16[1,128,128]{2,1,0:T(8,128)(2,1)S(1)}, u32[]{:S(2)}, u32[]{:S(2)}) collective-permute-start(bf16[1,128,128]{2,1,0:T(8,128)(2,1)S(1)} %get-tuple-element.47), channel_id=1, source_target_pairs={{0,1},{1,2},{2,3},{3,4},{4,5},{5,6},{6,7},{7,8},{8,9},{9,10},{10,1... | collective-permute-start | bytes 98312 | tf_op jit(solution)/shard_map/ppermute | solution.py:18
  39.6 10.0 %collective-permute-start.9 = (bf16[1,128,128]{2,1,0:T(8,128)(2,1)S(1)}, bf16[1,128,128]{2,1,0:T(8,128)(2,1)S(1)}, u32[]{:S(2)}, u32[]{:S(2)}) collective-permute-start(bf16[1,128,128]{2,1,0:T(8,128)(2,1)S(1)} %get-tuple-element.48), channel_id=1, source_target_pairs={{32,0},{64,32},{96,64},{33,1},{65,33},{97,65},{34,2},{66,34},{98,6... | collective-permute-start | bytes 98312 | tf_op jit(solution)/shard_map/ppermute | solution.py:19
  54.3 13.8 %collective-permute-start.12 = (bf16[1,128,128]{2,1,0:T(8,128)(2,1)S(1)}, bf16[1,128,128]{2,1,0:T(8,128)(2,1)S(1)}, u32[]{:S(2)}, u32[]{:S(2)}) collective-permute-start(bf16[1,128,128]{2,1,0:T(8,128)(2,1)S(1)} %get-tuple-element.45), channel_id=1, source_target_pairs={{0,128},{128,256},{256,384},{1,129},{129,257},{257,385},{2,130},{1... | collective-permute-start | bytes 98312 | tf_op jit(solution)/shard_map/ppermute | solution.py:18
  56.1 16.7 %collective-permute-start.17 = (bf16[1,128,128]{2,1,0:T(8,128)(2,1)S(1)}, bf16[1,128,128]{2,1,0:T(8,128)(2,1)S(1)}, u32[]{:S(2)}, u32[]{:S(2)}) collective-permute-start(bf16[1,128,128]{2,1,0:T(8,128)(2,1)S(1)} %get-tuple-element.40), channel_id=1, source_target_pairs={{1,0},{2,1},{3,2},{4,3},{5,4},{6,5},{7,6},{8,7},{9,8},{10,9},{11,1... | collective-permute-start | bytes 98312 | tf_op jit(solution)/shard_map/ppermute | solution.py:19
  60.4 12.4 %collective-permute-start.16 = (bf16[1,128,128]{2,1,0:T(8,128)(2,1)S(1)}, bf16[1,128,128]{2,1,0:T(8,128)(2,1)S(1)}, u32[]{:S(2)}, u32[]{:S(2)}) collective-permute-start(bf16[1,128,128]{2,1,0:T(8,128)(2,1)S(1)} %get-tuple-element.41), channel_id=1, source_target_pairs={{0,1},{1,2},{2,3},{3,4},{4,5},{5,6},{6,7},{7,8},{8,9},{9,10},{10,1... | collective-permute-start | bytes 98312 | tf_op jit(solution)/shard_map/ppermute | solution.py:18
  62.8 10.0 %collective-permute-start.15 = (bf16[1,128,128]{2,1,0:T(8,128)(2,1)S(1)}, bf16[1,128,128]{2,1,0:T(8,128)(2,1)S(1)}, u32[]{:S(2)}, u32[]{:S(2)}) collective-permute-start(bf16[1,128,128]{2,1,0:T(8,128)(2,1)S(1)} %get-tuple-element.42), channel_id=1, source_target_pairs={{32,0},{64,32},{96,64},{33,1},{65,33},{97,65},{34,2},{66,34},{98,6... | collective-permute-start | bytes 98312 | tf_op jit(solution)/shard_map/ppermute | solution.py:19
  64.1 8.7 %collective-permute-start.14 = (bf16[1,128,128]{2,1,0:T(8,128)(2,1)S(1)}, bf16[1,128,128]{2,1,0:T(8,128)(2,1)S(1)}, u32[]{:S(2)}, u32[]{:S(2)}) collective-permute-start(bf16[1,128,128]{2,1,0:T(8,128)(2,1)S(1)} %get-tuple-element.43), channel_id=1, source_target_pairs={{0,32},{32,64},{64,96},{1,33},{33,65},{65,97},{2,34},{34,66},{66,9... | collective-permute-start | bytes 98312 | tf_op jit(solution)/shard_map/ppermute | solution.py:18
  114.8 14.4 %collective-permute-start.18 = (bf16[1,128,128]{2,1,0:T(8,128)(2,1)S(1)}, bf16[1,128,128]{2,1,0:T(8,128)(2,1)S(1)}, u32[]{:S(2)}, u32[]{:S(2)}) collective-permute-start(bf16[1,128,128]{2,1,0:T(8,128)(2,1)S(1)} %get-tuple-element.39), channel_id=1, source_target_pairs={{0,128},{128,256},{256,384},{1,129},{129,257},{257,385},{2,130},{1... | collective-permute-start | bytes 98312 | tf_op jit(solution)/shard_map/ppermute | solution.py:18
  117.0 16.9 %collective-permute-start.23 = (bf16[1,128,128]{2,1,0:T(8,128)(2,1)S(1)}, bf16[1,128,128]{2,1,0:T(8,128)(2,1)S(1)}, u32[]{:S(2)}, u32[]{:S(2)}) collective-permute-start(bf16[1,128,128]{2,1,0:T(8,128)(2,1)S(1)} %get-tuple-element.34), channel_id=1, source_target_pairs={{1,0},{2,1},{3,2},{4,3},{5,4},{6,5},{7,6},{8,7},{9,8},{10,9},{11,1... | collective-permute-start | bytes 98312 | tf_op jit(solution)/shard_map/ppermute | solution.py:19
  121.7 12.1 %collective-permute-start.22 = (bf16[1,128,128]{2,1,0:T(8,128)(2,1)S(1)}, bf16[1,128,128]{2,1,0:T(8,128)(2,1)S(1)}, u32[]{:S(2)}, u32[]{:S(2)}) collective-permute-start(bf16[1,128,128]{2,1,0:T(8,128)(2,1)S(1)} %get-tuple-element.35), channel_id=1, source_target_pairs={{0,1},{1,2},{2,3},{3,4},{4,5},{5,6},{6,7},{7,8},{8,9},{9,10},{10,1... | collective-permute-start | bytes 98312 | tf_op jit(solution)/shard_map/ppermute | solution.py:18
  123.8 10.0 %collective-permute-start.21 = (bf16[1,128,128]{2,1,0:T(8,128)(2,1)S(1)}, bf16[1,128,128]{2,1,0:T(8,128)(2,1)S(1)}, u32[]{:S(2)}, u32[]{:S(2)}) collective-permute-start(bf16[1,128,128]{2,1,0:T(8,128)(2,1)S(1)} %get-tuple-element.36), channel_id=1, source_target_pairs={{32,0},{64,32},{96,64},{33,1},{65,33},{97,65},{34,2},{66,34},{98,6... | collective-permute-start | bytes 98312 | tf_op jit(solution)/shard_map/ppermute | solution.py:19
  125.1 8.7 %collective-permute-start.20 = (bf16[1,128,128]{2,1,0:T(8,128)(2,1)S(1)}, bf16[1,128,128]{2,1,0:T(8,128)(2,1)S(1)}, u32[]{:S(2)}, u32[]{:S(2)}) collective-permute-start(bf16[1,128,128]{2,1,0:T(8,128)(2,1)S(1)} %get-tuple-element.37), channel_id=1, source_target_pairs={{0,32},{32,64},{64,96},{1,33},{33,65},{65,97},{2,34},{34,66},{66,9... | collective-permute-start | bytes 98312 | tf_op jit(solution)/shard_map/ppermute | solution.py:18
  139.3 13.9 %collective-permute-start.24 = (bf16[1,128,128]{2,1,0:T(8,128)(2,1)S(1)}, bf16[1,128,128]{2,1,0:T(8,128)(2,1)S(1)}, u32[]{:S(2)}, u32[]{:S(2)}) collective-permute-start(bf16[1,128,128]{2,1,0:T(8,128)(2,1)S(1)} %get-tuple-element.33), channel_id=1, source_target_pairs={{0,128},{128,256},{256,384},{1,129},{129,257},{257,385},{2,130},{1... | collective-permute-start | bytes 98312 | tf_op jit(solution)/shard_map/ppermute | solution.py:18
  141.6 16.4 %collective-permute-start.29 = (bf16[1,128,128]{2,1,0:T(8,128)(2,1)S(1)}, bf16[1,128,128]{2,1,0:T(8,128)(2,1)S(1)}, u32[]{:S(2)}, u32[]{:S(2)}) collective-permute-start(bf16[1,128,128]{2,1,0:T(8,128)(2,1)S(1)} %get-tuple-element.28), channel_id=1, source_target_pairs={{1,0},{2,1},{3,2},{4,3},{5,4},{6,5},{7,6},{8,7},{9,8},{10,9},{11,1... | collective-permute-start | bytes 98312 | tf_op jit(solution)/shard_map/ppermute | solution.py:19
  145.8 12.1 %collective-permute-start.28 = (bf16[1,128,128]{2,1,0:T(8,128)(2,1)S(1)}, bf16[1,128,128]{2,1,0:T(8,128)(2,1)S(1)}, u32[]{:S(2)}, u32[]{:S(2)}) collective-permute-start(bf16[1,128,128]{2,1,0:T(8,128)(2,1)S(1)} %get-tuple-element.29), channel_id=1, source_target_pairs={{0,1},{1,2},{2,3},{3,4},{4,5},{5,6},{6,7},{7,8},{8,9},{9,10},{10,1... | collective-permute-start | bytes 98312 | tf_op jit(solution)/shard_map/ppermute | solution.py:18
  147.9 10.0 %collective-permute-start.27 = (bf16[1,128,128]{2,1,0:T(8,128)(2,1)S(1)}, bf16[1,128,128]{2,1,0:T(8,128)(2,1)S(1)}, u32[]{:S(2)}, u32[]{:S(2)}) collective-permute-start(bf16[1,128,128]{2,1,0:T(8,128)(2,1)S(1)} %get-tuple-element.30), channel_id=1, source_target_pairs={{32,0},{64,32},{96,64},{33,1},{65,33},{97,65},{34,2},{66,34},{98,6... | collective-permute-start | bytes 98312 | tf_op jit(solution)/shard_map/ppermute | solution.py:19
  149.2 8.7 %collective-permute-start.26 = (bf16[1,128,128]{2,1,0:T(8,128)(2,1)S(1)}, bf16[1,128,128]{2,1,0:T(8,128)(2,1)S(1)}, u32[]{:S(2)}, u32[]{:S(2)}) collective-permute-start(bf16[1,128,128]{2,1,0:T(8,128)(2,1)S(1)} %get-tuple-element.31), channel_id=1, source_target_pairs={{0,32},{32,64},{64,96},{1,33},{33,65},{65,97},{2,34},{34,66},{66,9... | collective-permute-start | bytes 98312 | tf_op jit(solution)/shard_map/ppermute | solution.py:18
  193.5 14.2 %collective-permute-start.30 = (bf16[1,128,128]{2,1,0:T(8,128)(2,1)S(1)}, bf16[1,128,128]{2,1,0:T(8,128)(2,1)S(1)}, u32[]{:S(2)}, u32[]{:S(2)}) collective-permute-start(bf16[1,128,128]{2,1,0:T(8,128)(2,1)S(1)} %get-tuple-element.27), channel_id=1, source_target_pairs={{0,128},{128,256},{256,384},{1,129},{129,257},{257,385},{2,130},{1... | collective-permute-start | bytes 98312 | tf_op jit(solution)/shard_map/ppermute | solution.py:18
  195.7 16.8 %collective-permute-start.35 = (bf16[1,128,128]{2,1,0:T(8,128)(2,1)S(1)}, bf16[1,128,128]{2,1,0:T(8,128)(2,1)S(1)}, u32[]{:S(2)}, u32[]{:S(2)}) collective-permute-start(bf16[1,128,128]{2,1,0:T(8,128)(2,1)S(1)} %get-tuple-element.22), channel_id=1, source_target_pairs={{1,0},{2,1},{3,2},{4,3},{5,4},{6,5},{7,6},{8,7},{9,8},{10,9},{11,1... | collective-permute-start | bytes 98312 | tf_op jit(solution)/shard_map/ppermute | solution.py:19
  200.3 12.2 %collective-permute-start.34 = (bf16[1,128,128]{2,1,0:T(8,128)(2,1)S(1)}, bf16[1,128,128]{2,1,0:T(8,128)(2,1)S(1)}, u32[]{:S(2)}, u32[]{:S(2)}) collective-permute-start(bf16[1,128,128]{2,1,0:T(8,128)(2,1)S(1)} %get-tuple-element.23), channel_id=1, source_target_pairs={{0,1},{1,2},{2,3},{3,4},{4,5},{5,6},{6,7},{7,8},{8,9},{9,10},{10,1... | collective-permute-start | bytes 98312 | tf_op jit(solution)/shard_map/ppermute | solution.py:18
  202.4 10.0 %collective-permute-start.33 = (bf16[1,128,128]{2,1,0:T(8,128)(2,1)S(1)}, bf16[1,128,128]{2,1,0:T(8,128)(2,1)S(1)}, u32[]{:S(2)}, u32[]{:S(2)}) collective-permute-start(bf16[1,128,128]{2,1,0:T(8,128)(2,1)S(1)} %get-tuple-element.24), channel_id=1, source_target_pairs={{32,0},{64,32},{96,64},{33,1},{65,33},{97,65},{34,2},{66,34},{98,6... | collective-permute-start | bytes 98312 | tf_op jit(solution)/shard_map/ppermute | solution.py:19
  217.9 13.9 %collective-permute-start.36 = (bf16[1,128,128]{2,1,0:T(8,128)(2,1)S(1)}, bf16[1,128,128]{2,1,0:T(8,128)(2,1)S(1)}, u32[]{:S(2)}, u32[]{:S(2)}) collective-permute-start(bf16[1,128,128]{2,1,0:T(8,128)(2,1)S(1)} %get-tuple-element.21), channel_id=1, source_target_pairs={{0,128},{128,256},{256,384},{1,129},{129,257},{257,385},{2,130},{1... | collective-permute-start | bytes 98312 | tf_op jit(solution)/shard_map/ppermute | solution.py:18
  220.2 16.4 %collective-permute-start.41 = (bf16[1,128,128]{2,1,0:T(8,128)(2,1)S(1)}, bf16[1,128,128]{2,1,0:T(8,128)(2,1)S(1)}, u32[]{:S(2)}, u32[]{:S(2)}) collective-permute-start(bf16[1,128,128]{2,1,0:T(8,128)(2,1)S(1)} %get-tuple-element.16), channel_id=1, source_target_pairs={{1,0},{2,1},{3,2},{4,3},{5,4},{6,5},{7,6},{8,7},{9,8},{10,9},{11,1... | collective-permute-start | bytes 98312 | tf_op jit(solution)/shard_map/ppermute | solution.py:19
  224.3 12.2 %collective-permute-start.40 = (bf16[1,128,128]{2,1,0:T(8,128)(2,1)S(1)}, bf16[1,128,128]{2,1,0:T(8,128)(2,1)S(1)}, u32[]{:S(2)}, u32[]{:S(2)}) collective-permute-start(bf16[1,128,128]{2,1,0:T(8,128)(2,1)S(1)} %get-tuple-element.17), channel_id=1, source_target_pairs={{0,1},{1,2},{2,3},{3,4},{4,5},{5,6},{6,7},{7,8},{8,9},{9,10},{10,1... | collective-permute-start | bytes 98312 | tf_op jit(solution)/shard_map/ppermute | solution.py:18
  226.5 10.0 %collective-permute-start.39 = (bf16[1,128,128]{2,1,0:T(8,128)(2,1)S(1)}, bf16[1,128,128]{2,1,0:T(8,128)(2,1)S(1)}, u32[]{:S(2)}, u32[]{:S(2)}) collective-permute-start(bf16[1,128,128]{2,1,0:T(8,128)(2,1)S(1)} %get-tuple-element.18), channel_id=1, source_target_pairs={{32,0},{64,32},{96,64},{33,1},{65,33},{97,65},{34,2},{66,34},{98,6... | collective-permute-start | bytes 98312 | tf_op jit(solution)/shard_map/ppermute | solution.py:19
  227.8 8.7 %collective-permute-start.38 = (bf16[1,128,128]{2,1,0:T(8,128)(2,1)S(1)}, bf16[1,128,128]{2,1,0:T(8,128)(2,1)S(1)}, u32[]{:S(2)}, u32[]{:S(2)}) collective-permute-start(bf16[1,128,128]{2,1,0:T(8,128)(2,1)S(1)} %get-tuple-element.19), channel_id=1, source_target_pairs={{0,32},{32,64},{64,96},{1,33},{33,65},{65,97},{2,34},{34,66},{66,9... | collective-permute-start | bytes 98312 | tf_op jit(solution)/shard_map/ppermute | solution.py:18
  (22 other events, 428.4 us)
where the time goes:
time: 267 us; the launch traced here: 265 us
  starting transfers between devices  112 us (42%)
  blocking collectives  91.9 us (34%)
  matrix products  26.5 us (10%)
  waiting for transfers between devices  24.4 us (9%)
  other arithmetic  7.4 us (3%)
    all_to_all x6, blocking collectives, sent_to_all(): return lax.all_to_all(copies, axis, split_axis=0, concat_axis=0, tiled=True)  91.9 us
    ppermute x21, starting transfers between devices, padded(): before = lax.ppermute(last, axis, up)  57.8 us
    ppermute x21, starting transfers between devices, padded(): after = lax.ppermute(initial, axis, down)  54.3 us
    ppermute x21, waiting for transfers between devices, padded(): after = lax.ppermute(initial, axis, down)  23.5 us
    dot_general x6, matrix products, spread(): jnp.dot(spread_table, values, precision=lax.Precision.HIGHEST, preferred_...  15.2 us
    dot_general x7, matrix products, own_faces(): jnp.dot(pick_table, values, preferred_element_type=jnp.float32)  11.4 us
  transfers between devices with their start and end apart: 42, of which 8 were waited for; matrix products, arithmetic and copies ran while one was open for 0% of the time, Pallas kernels for 0%

commit v1 on v0

v1 whole, which is shorter than its diff:
```python
import jax
import jax.numpy as jnp
from jax import lax
from jax.sharding import Mesh
from jax.sharding import PartitionSpec as P

GZ = ("gz_0", "gz_1")
AXES = (("gx", 0), ("gy", 2), (GZ, 4))
MOMENTS = 6


def swaps(devices, first):
    return [pair for i in range(first, devices - 1, 2) for pair in ((i, i + 1), (i + 1, i))]


def from_partners(faces):
    got = [None] * 6
    for axis, at in AXES:
        devices = lax.axis_size(axis)
        odd = lax.axis_index(axis) % 2 == 1
        low, high = faces[at], faces[at + 1]
        even_pairs = lax.ppermute(jnp.where(odd, low, high), axis, swaps(devices, 0))
        odd_pairs = lax.ppermute(jnp.where(odd, high, low), axis, swaps(devices, 1))
        got[at] = jnp.where(odd, even_pairs, odd_pairs)
        got[at + 1] = jnp.where(odd, odd_pairs, even_pairs)
    return jnp.stack(got)


def from_everyone(value, axis):
    copies = jnp.broadcast_to(value, (lax.axis_size(axis), *value.shape))
    return lax.all_to_all(copies, axis, split_axis=0, concat_axis=0, tiled=True)


def totals(moments, scale):
    for axis in (("gx", "gy"), GZ):
        scale = jnp.broadcast_to(scale, moments.shape[1:])
        packed = jnp.concatenate([moments, scale[None]])
        everyone = from_everyone(packed, axis)
        scales = everyone[:, MOMENTS]
        scale = jnp.max(scales, axis=0)
        ratio, power, sums = scales / scale, 1.0, []
        for k in range(MOMENTS):
            sums.append(jnp.sum(everyone[:, k] * power, axis=0))
            power = power * ratio
        moments = jnp.stack(sums)
    return moments, scale


def weights_of(moments):
    c0, c1, c2, c3, c4, c5 = [moments[k] for k in range(MOMENTS)]
    l10, l20 = c2 / c1, c3 / c1
    d1 = c3 - l10 * c2
    e21 = c4 - l10 * c3
    l21 = e21 / d1
    d2 = c5 - l20 * c3 - l21 * e21
    y1 = c1 - l10 * c0
    y2 = c2 - l20 * c0 - l21 * y1
    w2 = y2 / d2
    w1 = y1 / d1 - l21 * w2
    w0 = c0 / c1 - l10 * w1 - l20 * w2
    return w0, w1, w2


def shards(displacement, flexibility, schur, face_rows, multiplicity):
    width = flexibility.shape[-1]
    loads = displacement.shape[-1]
    slots = face_rows.shape[-1]
    face_len = slots // 6
    displaced = displacement.reshape(width, loads)
    flex_op = flexibility.reshape(width, width)
    schur_op = schur.reshape(width, width)
    rows = face_rows.reshape(slots, 1)
    weight = 2.0 / multiplicity.reshape(slots, 1).astype(jnp.float32)
    columns = jnp.arange(width, dtype=jnp.int32).reshape(1, width)
    here = rows == columns
    pick = here.astype(jnp.bfloat16)
    weighted_pick = jnp.where(here, weight, 0.0).astype(jnp.bfloat16)

    def minus_partner(own):
        faces = own.reshape(6, face_len, loads)
        partners = from_partners(faces)
        return (faces.astype(jnp.float32) - partners.astype(jnp.float32)).reshape(slots, loads)

    def on_slots(table, op):
        half = jnp.dot(table, op, preferred_element_type=jnp.float32).astype(jnp.bfloat16)
        return lax.dot_general(
            half, table, (((1,), (1,)), ((), ())), preferred_element_type=jnp.float32
        ).astype(jnp.bfloat16)

    def apply(op, values):
        high = lax.reduce_precision(values, 8, 7)
        parts = jnp.concatenate([high, values - high], axis=1).astype(jnp.bfloat16)
        both = jnp.dot(op, parts, preferred_element_type=jnp.float32)
        return both[:, :loads] + both[:, loads:]

    def dots(left, right):
        return jnp.sum(left * right, axis=0)

    def largest_diagonal(op):
        on = jnp.arange(width).reshape(width, 1) == columns
        return jnp.max(jnp.where(on, op, 0).astype(jnp.float32))

    picked = jnp.dot(pick, displaced, preferred_element_type=jnp.float32).astype(jnp.bfloat16)
    residual = minus_partner(picked)
    schur_slots = on_slots(weighted_pick, schur_op)
    flex_slots = on_slots(pick, flex_op)
    scale = largest_diagonal(flex_op) * largest_diagonal(schur_op)
    down = 1.0 / scale

    smooth0 = apply(schur_slots, residual)
    basis0 = minus_partner(smooth0)
    bent0 = apply(flex_slots, basis0)
    smooth1 = apply(schur_slots, minus_partner(bent0))
    basis1 = minus_partner(smooth1)
    bent1 = apply(flex_slots, basis1)
    smooth2 = apply(schur_slots, minus_partner(bent1))
    basis2 = minus_partner(smooth2)
    bent2 = apply(flex_slots, basis2)

    near1, near2 = basis1 * down, basis2 * down * down
    moments = jnp.stack(
        [
            dots(residual, smooth0),
            dots(basis0, bent0 * down),
            dots(near1, bent0 * down),
            dots(near1, bent1 * down * down),
            dots(near2, bent1 * down * down),
            dots(near2, bent2 * down * down * down),
        ]
    )
    moments, common = totals(moments, scale)
    w0, w1, w2 = weights_of(moments)
    up = 1.0 / common
    result = (
        (w0 * up) * basis0
        + (w1 * up) * (up * basis1)
        + (w2 * up) * (up * (up * basis2))
    )
    return result.reshape(1, 1, 1, slots, loads)


def solution(mesh):
    torus = Mesh(
        mesh.devices.reshape(mesh.shape["gx"], mesh.shape["gy"], 16, 2),
        ("gx", "gy", "gz_0", "gz_1"),
    )
    return jax.shard_map(
        shards,
        mesh=torus,
        in_specs=(
            P("gx", "gy", GZ, None, None),
            P("gx", "gy", GZ, None, None),
            P("gx", "gy", GZ, None, None),
            P("gx", "gy", GZ, None),
            P("gx", "gy", GZ, None),
        ),
        out_specs=P("gx", "gy", GZ, None, None),
        check_vma=False,
    )
```

time: 267 us -> 179 us (0.67)
  blocking collectives: 91.9 us -> 50.6 us
  matrix products: 26.5 us -> 9.02 us
  starting transfers between devices: 112 us -> 95 us
  waiting for transfers between devices: 24.4 us -> 13.4 us
    all_to_all x6 -> x2, blocking collectives: 91.9 us -> 50.6 us  [from_everyone(): return lax.all_to_all(copies, axis, split_axis=0, concat_axis=0, tiled=True)]
    dot_general x13 -> x9, matrix products: 26.5 us -> 9.02 us  [the longest x2 5.6 us: on_slots(): lax.dot_general(half, table, (((1,), (1,)), ((), ())), preferred_element_...]
    ppermute x42 -> x36, starting transfers between devices: 112 us -> 95 us  [the longest x18 65.1 us: from_partners(): lax.ppermute(jnp.where(odd, low, high), axis, swaps(devices, 0))]
    ppermute x42 -> x36, waiting for transfers between devices: 24.4 us -> 13.4 us  [the longest x18 13.3 us: from_partners(): odd_pairs = lax.ppermute(jnp.where(odd, high, low), axis, swaps(devices, 1))]
  transfers between devices with their start and end apart: 42 -> 36, of which waited for: 8 -> 6; matrix products, arithmetic and copies ran while one was open for 0% -> 4% of each run, Pallas kernels for 0% -> 0%
where the time goes in v1:
time: 179 us; the launch traced here: 178 us
  starting transfers between devices  95 us (53%)
  blocking collectives  50.6 us (28%)
  waiting for transfers between devices  13.4 us (7%)
  matrix products  9.02 us (5%)
  other arithmetic  5.71 us (3%)
  between operations  2.5 us (1%)
  local copies, waits for them, and re-layouts  1.99 us (1%)
    ppermute x18, starting transfers between devices, from_partners(): lax.ppermute(jnp.where(odd, low, high), axis, swaps(devices, 0))  65.1 us
    all_to_all x2, blocking collectives, from_everyone(): return lax.all_to_all(copies, axis, split_axis=0, concat_axis=0, tiled=True)  50.6 us
    ppermute x18, starting transfers between devices, from_partners(): odd_pairs = lax.ppermute(jnp.where(odd, high, low), axis, swaps(devices, 1))  29.9 us
    ppermute x18, waiting for transfers between devices, from_partners(): odd_pairs = lax.ppermute(jnp.where(odd, high, low), axis, swaps(devices, 1))  13.3 us
    dot_general x2, matrix products, on_slots(): lax.dot_general(half, table, (((1,), (1,)), ((), ())), preferred_element_...  5.6 us
  transfers between devices with their start and end apart: 36, of which 6 were waited for; matrix products, arithmetic and copies ran while one was open for 4% of the time, Pallas kernels for 0%

profile of v1, /device:TPU:1, one launch (start us, length us, event | category | flops | bytes accessed | tf_op | source)
XLA Modules:
  0.0 178.2 jit_solution(18179820608384148177)
XLA Ops:
  1.5 3.9 %collective-permute-start = (bf16[128,128]{1,0:T(8,128)(2,1)S(1)}, bf16[128,128]{1,0:T(8,128)(2,1)S(1)}, u32[]{:S(2)}, u32[]{:S(2)}) collective-permute-start(bf16[128,128]{1,0:T(8,128)(2,1)S(1)} %get-tuple-element.71), channel_id=1, source_target_pairs={{0,128},{128,0},{256,384},{384,256},{1,129},{129,1},{257,385},{385... | collective-permute-start | bytes 98312 | tf_op jit(solution)/shard_map/ppermute | solution.py:22
  6.1 3.2 %collective-permute-start.2 = (bf16[128,128]{1,0:T(8,128)(2,1)S(1)}, bf16[128,128]{1,0:T(8,128)(2,1)S(1)}, u32[]{:S(2)}, u32[]{:S(2)}) collective-permute-start(bf16[128,128]{1,0:T(8,128)(2,1)S(1)} %get-tuple-element.69), channel_id=1, source_target_pairs={{0,32},{32,0},{64,96},{96,64},{1,33},{33,1},{65,97},{97,65},{2,34}... | collective-permute-start | bytes 98312 | tf_op jit(solution)/shard_map/ppermute | solution.py:22
  10.0 5.4 %collective-permute-start.4 = (bf16[128,128]{1,0:T(8,128)(2,1)S(1)}, bf16[128,128]{1,0:T(8,128)(2,1)S(1)}, u32[]{:S(2)}, u32[]{:S(2)}) collective-permute-start(bf16[128,128]{1,0:T(8,128)(2,1)S(1)} %get-tuple-element.73), channel_id=1, source_target_pairs={{0,1},{1,0},{2,3},{3,2},{4,5},{5,4},{6,7},{7,6},{8,9},{9,8},{10,11... | collective-permute-start | bytes 98312 | tf_op jit(solution)/shard_map/ppermute | solution.py:22
  15.5 2.2 %convolution_convert_fusion = bf16[768,768]{1,0:T(8,128)(2,1)S(1)} fusion(bf16[1,1,1,768,768]{4,3,2,1,0:T(8,128)(2,1)S(1)} %copy-done.10, bf16[768]{0:T(1024)(128)(2,1)S(1)} %divide_reduce_fusion, s32[768]{0:T(1024)S(1)} %reduce.6), kind=kOutput, calls=%fused_computation.10 | convolution fusion | flops 1815478272 | bytes 2363904 | tf_op jit(solution)/shard_map/dot_general | solution.py:86
  17.7 1.9 %collective-permute-start.5 = (bf16[128,128]{1,0:T(8,128)(2,1)S(1)}, bf16[128,128]{1,0:T(8,128)(2,1)S(1)}, u32[]{:S(2)}, u32[]{:S(2)}) collective-permute-start(bf16[128,128]{1,0:T(8,128)(2,1)S(1)} %get-tuple-element.68), channel_id=1, source_target_pairs={{1,2},{2,1},{3,4},{4,3},{5,6},{6,5},{7,8},{8,7},{9,10},{10,9},{11,... | collective-permute-start | bytes 98312 | tf_op jit(solution)/shard_map/ppermute | solution.py:23
  19.8 3.2 %collective-permute-done.5 = bf16[128,128]{1,0:T(8,128)(2,1)S(1)} collective-permute-done((bf16[128,128]{1,0:T(8,128)(2,1)S(1)}, bf16[128,128]{1,0:T(8,128)(2,1)S(1)}, u32[]{:S(2)}, u32[]{:S(2)}) %collective-permute-start.5) | collective-permute-done | bytes 32800 | tf_op jit(solution)/shard_map/ppermute | solution.py:23
  23.8 4.9 %collective-permute-start.6 = (f32[128,128]{1,0:T(8,128)S(1)}, f32[128,128]{1,0:T(8,128)S(1)}, u32[]{:S(2)}, u32[]{:S(2)}) collective-permute-start(f32[128,128]{1,0:T(8,128)S(1)} %get-tuple-element.64), channel_id=1, source_target_pairs={{0,128},{128,0},{256,384},{384,256},{1,129},{129,1},{257,385},{385... | collective-permute-start | bytes 196616 | tf_op jit(solution)/shard_map/ppermute | solution.py:22
  29.4 3.4 %fusion.6 = bf16[768,768]{1,0:T(8,128)(2,1)S(1)} fusion(s32[768]{0:T(1024)S(1)} %reduce.6, bf16[1,1,1,768,768]{4,3,2,1,0:T(8,128)(2,1)} %param.6), kind=kOutput, calls=%fused_computation.9 | convolution fusion | flops 1814298624 | bytes 2362368 | tf_op jit(solution)/shard_map/dot_general | solution.py:86
  32.8 4.9 %collective-permute-start.8 = (f32[128,128]{1,0:T(8,128)S(1)}, f32[128,128]{1,0:T(8,128)S(1)}, u32[]{:S(2)}, u32[]{:S(2)}) collective-permute-start(f32[128,128]{1,0:T(8,128)S(1)} %get-tuple-element.62), channel_id=1, source_target_pairs={{0,32},{32,0},{64,96},{96,64},{1,33},{33,1},{65,97},{97,65},{2,34}... | collective-permute-start | bytes 196616 | tf_op jit(solution)/shard_map/ppermute | solution.py:22
  38.4 1.9 %collective-permute-start.10 = (f32[128,128]{1,0:T(8,128)S(1)}, f32[128,128]{1,0:T(8,128)S(1)}, u32[]{:S(2)}, u32[]{:S(2)}) collective-permute-start(f32[128,128]{1,0:T(8,128)S(1)} %get-tuple-element.61), channel_id=1, source_target_pairs={{0,1},{1,0},{2,3},{3,2},{4,5},{5,4},{6,7},{7,6},{8,9},{9,8},{10,11... | collective-permute-start | bytes 196616 | tf_op jit(solution)/shard_map/ppermute | solution.py:22
  40.3 3.2 %collective-permute-start.11 = (f32[128,128]{1,0:T(8,128)S(1)}, f32[128,128]{1,0:T(8,128)S(1)}, u32[]{:S(2)}, u32[]{:S(2)}) collective-permute-start(f32[128,128]{1,0:T(8,128)S(1)} %get-tuple-element.60), channel_id=1, source_target_pairs={{1,2},{2,1},{3,4},{4,3},{5,6},{6,5},{7,8},{8,7},{9,10},{10,9},{11,... | collective-permute-start | bytes 196616 | tf_op jit(solution)/shard_map/ppermute | solution.py:23
  43.7 2.3 %collective-permute-done.11 = f32[128,128]{1,0:T(8,128)S(1)} collective-permute-done((f32[128,128]{1,0:T(8,128)S(1)}, f32[128,128]{1,0:T(8,128)S(1)}, u32[]{:S(2)}, u32[]{:S(2)}) %collective-permute-start.11) | collective-permute-done | bytes 65568 | tf_op jit(solution)/shard_map/ppermute | solution.py:23
  46.6 4.9 %collective-permute-start.12 = (f32[128,128]{1,0:T(8,128)S(1)}, f32[128,128]{1,0:T(8,128)S(1)}, u32[]{:S(2)}, u32[]{:S(2)}) collective-permute-start(f32[128,128]{1,0:T(8,128)S(1)} %get-tuple-element.58), channel_id=1, source_target_pairs={{0,128},{128,0},{256,384},{384,256},{1,129},{129,1},{257,385},{385... | collective-permute-start | bytes 196616 | tf_op jit(solution)/shard_map/ppermute | solution.py:22
  52.2 4.9 %collective-permute-start.14 = (f32[128,128]{1,0:T(8,128)S(1)}, f32[128,128]{1,0:T(8,128)S(1)}, u32[]{:S(2)}, u32[]{:S(2)}) collective-permute-start(f32[128,128]{1,0:T(8,128)S(1)} %get-tuple-element.56), channel_id=1, source_target_pairs={{0,32},{32,0},{64,96},{96,64},{1,33},{33,1},{65,97},{97,65},{2,34}... | collective-permute-start | bytes 196616 | tf_op jit(solution)/shard_map/ppermute | solution.py:22
  57.8 1.9 %collective-permute-start.16 = (f32[128,128]{1,0:T(8,128)S(1)}, f32[128,128]{1,0:T(8,128)S(1)}, u32[]{:S(2)}, u32[]{:S(2)}) collective-permute-start(f32[128,128]{1,0:T(8,128)S(1)} %get-tuple-element.55), channel_id=1, source_target_pairs={{0,1},{1,0},{2,3},{3,2},{4,5},{5,4},{6,7},{7,6},{8,9},{9,8},{10,11... | collective-permute-start | bytes 196616 | tf_op jit(solution)/shard_map/ppermute | solution.py:22
  59.8 3.0 %collective-permute-start.17 = (f32[128,128]{1,0:T(8,128)S(1)}, f32[128,128]{1,0:T(8,128)S(1)}, u32[]{:S(2)}, u32[]{:S(2)}) collective-permute-start(f32[128,128]{1,0:T(8,128)S(1)} %get-tuple-element.54), channel_id=1, source_target_pairs={{1,2},{2,1},{3,4},{4,3},{5,6},{6,5},{7,8},{8,7},{9,10},{10,9},{11,... | collective-permute-start | bytes 196616 | tf_op jit(solution)/shard_map/ppermute | solution.py:23
  62.9 2.4 %collective-permute-done.17 = f32[128,128]{1,0:T(8,128)S(1)} collective-permute-done((f32[128,128]{1,0:T(8,128)S(1)}, f32[128,128]{1,0:T(8,128)S(1)}, u32[]{:S(2)}, u32[]{:S(2)}) %collective-permute-start.17) | collective-permute-done | bytes 65568 | tf_op jit(solution)/shard_map/ppermute | solution.py:23
  66.0 3.4 %collective-permute-start.18 = (f32[128,128]{1,0:T(8,128)S(1)}, f32[128,128]{1,0:T(8,128)S(1)}, u32[]{:S(2)}, u32[]{:S(2)}) collective-permute-start(f32[128,128]{1,0:T(8,128)S(1)} %get-tuple-element.52), channel_id=1, source_target_pairs={{0,128},{128,0},{256,384},{384,256},{1,129},{129,1},{257,385},{385... | collective-permute-start | bytes 196616 | tf_op jit(solution)/shard_map/ppermute | solution.py:22
  70.1 3.4 %collective-permute-start.20 = (f32[128,128]{1,0:T(8,128)S(1)}, f32[128,128]{1,0:T(8,128)S(1)}, u32[]{:S(2)}, u32[]{:S(2)}) collective-permute-start(f32[128,128]{1,0:T(8,128)S(1)} %get-tuple-element.50), channel_id=1, source_target_pairs={{0,32},{32,0},{64,96},{96,64},{1,33},{33,1},{65,97},{97,65},{2,34}... | collective-permute-start | bytes 196616 | tf_op jit(solution)/shard_map/ppermute | solution.py:22
  74.1 1.9 %collective-permute-start.22 = (f32[128,128]{1,0:T(8,128)S(1)}, f32[128,128]{1,0:T(8,128)S(1)}, u32[]{:S(2)}, u32[]{:S(2)}) collective-permute-start(f32[128,128]{1,0:T(8,128)S(1)} %get-tuple-element.49), channel_id=1, source_target_pairs={{0,1},{1,0},{2,3},{3,2},{4,5},{5,4},{6,7},{7,6},{8,9},{9,8},{10,11... | collective-permute-start | bytes 196616 | tf_op jit(solution)/shard_map/ppermute | solution.py:22
  76.1 4.2 %collective-permute-start.23 = (f32[128,128]{1,0:T(8,128)S(1)}, f32[128,128]{1,0:T(8,128)S(1)}, u32[]{:S(2)}, u32[]{:S(2)}) collective-permute-start(f32[128,128]{1,0:T(8,128)S(1)} %get-tuple-element.48), channel_id=1, source_target_pairs={{1,2},{2,1},{3,4},{4,3},{5,6},{6,5},{7,8},{8,7},{9,10},{10,9},{11,... | collective-permute-start | bytes 196616 | tf_op jit(solution)/shard_map/ppermute | solution.py:23
  83.1 4.2 %collective-permute-start.24 = (f32[128,128]{1,0:T(8,128)S(1)}, f32[128,128]{1,0:T(8,128)S(1)}, u32[]{:S(2)}, u32[]{:S(2)}) collective-permute-start(f32[128,128]{1,0:T(8,128)S(1)} %get-tuple-element.46), channel_id=1, source_target_pairs={{0,128},{128,0},{256,384},{384,256},{1,129},{129,1},{257,385},{385... | collective-permute-start | bytes 196616 | tf_op jit(solution)/shard_map/ppermute | solution.py:22
  87.9 4.2 %collective-permute-start.26 = (f32[128,128]{1,0:T(8,128)S(1)}, f32[128,128]{1,0:T(8,128)S(1)}, u32[]{:S(2)}, u32[]{:S(2)}) collective-permute-start(f32[128,128]{1,0:T(8,128)S(1)} %get-tuple-element.44), channel_id=1, source_target_pairs={{0,32},{32,0},{64,96},{96,64},{1,33},{33,1},{65,97},{97,65},{2,34}... | collective-permute-start | bytes 196616 | tf_op jit(solution)/shard_map/ppermute | solution.py:22
  92.8 1.9 %collective-permute-start.28 = (f32[128,128]{1,0:T(8,128)S(1)}, f32[128,128]{1,0:T(8,128)S(1)}, u32[]{:S(2)}, u32[]{:S(2)}) collective-permute-start(f32[128,128]{1,0:T(8,128)S(1)} %get-tuple-element.43), channel_id=1, source_target_pairs={{0,1},{1,0},{2,3},{3,2},{4,5},{5,4},{6,7},{7,6},{8,9},{9,8},{10,11... | collective-permute-start | bytes 196616 | tf_op jit(solution)/shard_map/ppermute | solution.py:22
  94.8 4.2 %collective-permute-start.29 = (f32[128,128]{1,0:T(8,128)S(1)}, f32[128,128]{1,0:T(8,128)S(1)}, u32[]{:S(2)}, u32[]{:S(2)}) collective-permute-start(f32[128,128]{1,0:T(8,128)S(1)} %get-tuple-element.42), channel_id=1, source_target_pairs={{1,2},{2,1},{3,4},{4,3},{5,6},{6,5},{7,8},{8,7},{9,10},{10,9},{11,... | collective-permute-start | bytes 196616 | tf_op jit(solution)/shard_map/ppermute | solution.py:23
  103.1 3.7 %collective-permute-start.30 = (f32[128,128]{1,0:T(8,128)}, f32[128,128]{1,0:T(8,128)S(1)}, u32[]{:S(2)}, u32[]{:S(2)}) collective-permute-start(f32[128,128]{1,0:T(8,128)} %get-tuple-element.40), channel_id=1, source_target_pairs={{0,128},{128,0},{256,384},{384,256},{1,129},{129,1},{257,385},{385... | collective-permute-start | bytes 196616 | tf_op jit(solution)/shard_map/ppermute | solution.py:22
  110.1 4.6 %collective-permute-start.32 = (f32[128,128]{1,0:T(8,128)}, f32[128,128]{1,0:T(8,128)S(1)}, u32[]{:S(2)}, u32[]{:S(2)}) collective-permute-start(f32[128,128]{1,0:T(8,128)} %get-tuple-element.38), channel_id=1, source_target_pairs={{0,32},{32,0},{64,96},{96,64},{1,33},{33,1},{65,97},{97,65},{2,34}... | collective-permute-start | bytes 196616 | tf_op jit(solution)/shard_map/ppermute | solution.py:22
  115.3 1.9 %collective-permute-start.34 = (f32[128,128]{1,0:T(8,128)}, f32[128,128]{1,0:T(8,128)S(1)}, u32[]{:S(2)}, u32[]{:S(2)}) collective-permute-start(f32[128,128]{1,0:T(8,128)} %get-tuple-element.37), channel_id=1, source_target_pairs={{0,1},{1,0},{2,3},{3,2},{4,5},{5,4},{6,7},{7,6},{8,9},{9,8},{10,11... | collective-permute-start | bytes 196616 | tf_op jit(solution)/shard_map/ppermute | solution.py:22
  117.3 5.4 %collective-permute-start.35 = (f32[128,128]{1,0:T(8,128)S(1)}, f32[128,128]{1,0:T(8,128)S(1)}, u32[]{:S(2)}, u32[]{:S(2)}) collective-permute-start(f32[128,128]{1,0:T(8,128)S(1)} %get-tuple-element.36), channel_id=1, source_target_pairs={{1,2},{2,1},{3,4},{4,3},{5,6},{6,5},{7,8},{8,7},{9,10},{10,9},{11,... | collective-permute-start | bytes 196616 | tf_op jit(solution)/shard_map/ppermute | solution.py:23
  122.8 1.8 %collective-permute-done.35 = f32[128,128]{1,0:T(8,128)S(1)} collective-permute-done((f32[128,128]{1,0:T(8,128)S(1)}, f32[128,128]{1,0:T(8,128)S(1)}, u32[]{:S(2)}, u32[]{:S(2)}) %collective-permute-start.35) | collective-permute-done | bytes 65568 | tf_op jit(solution)/shard_map/ppermute | solution.py:23
  126.3 13.6 %all_to_all.10 = f32[16,7,128]{2,1,0:T(8,128)S(1)} all-to-all(f32[16,7,128]{2,1,0:T(8,128)S(1)} %broadcast_in_dim.37), channel_id=1, replica_groups=mesh['gx'=4,'gy'=4,'gz_0'=16,'gz_1'=2] {'gx','gy'}, dimensions={0} | all-to-all | bytes 114688 | tf_op jit(solution)/shard_map/all_to_all | solution.py:31
  140.1 37.0 %all_to_all.11 = f32[32,7,128]{2,1,0:T(8,128)S(1)} all-to-all(f32[32,7,128]{2,1,0:T(8,128)S(1)} %broadcast_in_dim.39), channel_id=1, replica_groups=mesh['gx'=4,'gy'=4,'gz_0'=16,'gz_1'=2] {'gz_0','gz_1'}, dimensions={0} | all-to-all | bytes 229376 | tf_op jit(solution)/shard_map/all_to_all | solution.py:31
  (155 shorter events, 22.8 us)
Async XLA Ops:
  1.5 16.2 %collective-permute-start = (bf16[128,128]{1,0:T(8,128)(2,1)S(1)}, bf16[128,128]{1,0:T(8,128)(2,1)S(1)}, u32[]{:S(2)}, u32[]{:S(2)}) collective-permute-start(bf16[128,128]{1,0:T(8,128)(2,1)S(1)} %get-tuple-element.71), channel_id=1, source_target_pairs={{0,128},{128,0},{256,384},{384,256},{1,129},{129,1},{257,385},{385... | collective-permute-start | bytes 98312 | tf_op jit(solution)/shard_map/ppermute | solution.py:22
  5.5 14.2 %collective-permute-start.1 = (bf16[128,128]{1,0:T(8,128)(2,1)S(1)}, bf16[128,128]{1,0:T(8,128)(2,1)S(1)}, u32[]{:S(2)}, u32[]{:S(2)}) collective-permute-start(bf16[128,128]{1,0:T(8,128)(2,1)S(1)} %get-tuple-element.72), channel_id=1, source_target_pairs={{128,256},{256,128},{129,257},{257,129},{130,258},{258,130},{131,2... | collective-permute-start | bytes 98312 | tf_op jit(solution)/shard_map/ppermute | solution.py:23
  6.1 13.6 %collective-permute-start.2 = (bf16[128,128]{1,0:T(8,128)(2,1)S(1)}, bf16[128,128]{1,0:T(8,128)(2,1)S(1)}, u32[]{:S(2)}, u32[]{:S(2)}) collective-permute-start(bf16[128,128]{1,0:T(8,128)(2,1)S(1)} %get-tuple-element.69), channel_id=1, source_target_pairs={{0,32},{32,0},{64,96},{96,64},{1,33},{33,1},{65,97},{97,65},{2,34}... | collective-permute-start | bytes 98312 | tf_op jit(solution)/shard_map/ppermute | solution.py:22
  9.4 10.4 %collective-permute-start.3 = (bf16[128,128]{1,0:T(8,128)(2,1)S(1)}, bf16[128,128]{1,0:T(8,128)(2,1)S(1)}, u32[]{:S(2)}, u32[]{:S(2)}) collective-permute-start(bf16[128,128]{1,0:T(8,128)(2,1)S(1)} %get-tuple-element.70), channel_id=1, source_target_pairs={{32,64},{64,32},{33,65},{65,33},{34,66},{66,34},{35,67},{67,35},{3... | collective-permute-start | bytes 98312 | tf_op jit(solution)/shard_map/ppermute | solution.py:23
  10.0 9.8 %collective-permute-start.4 = (bf16[128,128]{1,0:T(8,128)(2,1)S(1)}, bf16[128,128]{1,0:T(8,128)(2,1)S(1)}, u32[]{:S(2)}, u32[]{:S(2)}) collective-permute-start(bf16[128,128]{1,0:T(8,128)(2,1)S(1)} %get-tuple-element.73), channel_id=1, source_target_pairs={{0,1},{1,0},{2,3},{3,2},{4,5},{5,4},{6,7},{7,6},{8,9},{9,8},{10,11... | collective-permute-start | bytes 98312 | tf_op jit(solution)/shard_map/ppermute | solution.py:22
  23.8 16.5 %collective-permute-start.6 = (f32[128,128]{1,0:T(8,128)S(1)}, f32[128,128]{1,0:T(8,128)S(1)}, u32[]{:S(2)}, u32[]{:S(2)}) collective-permute-start(f32[128,128]{1,0:T(8,128)S(1)} %get-tuple-element.64), channel_id=1, source_target_pairs={{0,128},{128,0},{256,384},{384,256},{1,129},{129,1},{257,385},{385... | collective-permute-start | bytes 196616 | tf_op jit(solution)/shard_map/ppermute | solution.py:22
  28.7 14.8 %collective-permute-start.7 = (f32[128,128]{1,0:T(8,128)S(1)}, f32[128,128]{1,0:T(8,128)S(1)}, u32[]{:S(2)}, u32[]{:S(2)}) collective-permute-start(f32[128,128]{1,0:T(8,128)S(1)} %get-tuple-element.65), channel_id=1, source_target_pairs={{128,256},{256,128},{129,257},{257,129},{130,258},{258,130},{131,2... | collective-permute-start | bytes 196616 | tf_op jit(solution)/shard_map/ppermute | solution.py:23
  32.8 10.8 %collective-permute-start.8 = (f32[128,128]{1,0:T(8,128)S(1)}, f32[128,128]{1,0:T(8,128)S(1)}, u32[]{:S(2)}, u32[]{:S(2)}) collective-permute-start(f32[128,128]{1,0:T(8,128)S(1)} %get-tuple-element.62), channel_id=1, source_target_pairs={{0,32},{32,0},{64,96},{96,64},{1,33},{33,1},{65,97},{97,65},{2,34}... | collective-permute-start | bytes 196616 | tf_op jit(solution)/shard_map/ppermute | solution.py:22
  37.7 5.9 %collective-permute-start.9 = (f32[128,128]{1,0:T(8,128)S(1)}, f32[128,128]{1,0:T(8,128)S(1)}, u32[]{:S(2)}, u32[]{:S(2)}) collective-permute-start(f32[128,128]{1,0:T(8,128)S(1)} %get-tuple-element.63), channel_id=1, source_target_pairs={{32,64},{64,32},{33,65},{65,33},{34,66},{66,34},{35,67},{67,35},{3... | collective-permute-start | bytes 196616 | tf_op jit(solution)/shard_map/ppermute | solution.py:23
  40.3 5.6 %collective-permute-start.11 = (f32[128,128]{1,0:T(8,128)S(1)}, f32[128,128]{1,0:T(8,128)S(1)}, u32[]{:S(2)}, u32[]{:S(2)}) collective-permute-start(f32[128,128]{1,0:T(8,128)S(1)} %get-tuple-element.60), channel_id=1, source_target_pairs={{1,2},{2,1},{3,4},{4,3},{5,6},{6,5},{7,8},{8,7},{9,10},{10,9},{11,... | collective-permute-start | bytes 196616 | tf_op jit(solution)/shard_map/ppermute | solution.py:23
  46.6 13.1 %collective-permute-start.12 = (f32[128,128]{1,0:T(8,128)S(1)}, f32[128,128]{1,0:T(8,128)S(1)}, u32[]{:S(2)}, u32[]{:S(2)}) collective-permute-start(f32[128,128]{1,0:T(8,128)S(1)} %get-tuple-element.58), channel_id=1, source_target_pairs={{0,128},{128,0},{256,384},{384,256},{1,129},{129,1},{257,385},{385... | collective-permute-start | bytes 196616 | tf_op jit(solution)/shard_map/ppermute | solution.py:22
  51.6 11.2 %collective-permute-start.13 = (f32[128,128]{1,0:T(8,128)S(1)}, f32[128,128]{1,0:T(8,128)S(1)}, u32[]{:S(2)}, u32[]{:S(2)}) collective-permute-start(f32[128,128]{1,0:T(8,128)S(1)} %get-tuple-element.59), channel_id=1, source_target_pairs={{128,256},{256,128},{129,257},{257,129},{130,258},{258,130},{131,2... | collective-permute-start | bytes 196616 | tf_op jit(solution)/shard_map/ppermute | solution.py:23
  52.2 10.6 %collective-permute-start.14 = (f32[128,128]{1,0:T(8,128)S(1)}, f32[128,128]{1,0:T(8,128)S(1)}, u32[]{:S(2)}, u32[]{:S(2)}) collective-permute-start(f32[128,128]{1,0:T(8,128)S(1)} %get-tuple-element.56), channel_id=1, source_target_pairs={{0,32},{32,0},{64,96},{96,64},{1,33},{33,1},{65,97},{97,65},{2,34}... | collective-permute-start | bytes 196616 | tf_op jit(solution)/shard_map/ppermute | solution.py:22
  57.1 5.7 %collective-permute-start.15 = (f32[128,128]{1,0:T(8,128)S(1)}, f32[128,128]{1,0:T(8,128)S(1)}, u32[]{:S(2)}, u32[]{:S(2)}) collective-permute-start(f32[128,128]{1,0:T(8,128)S(1)} %get-tuple-element.57), channel_id=1, source_target_pairs={{32,64},{64,32},{33,65},{65,33},{34,66},{66,34},{35,67},{67,35},{3... | collective-permute-start | bytes 196616 | tf_op jit(solution)/shard_map/ppermute | solution.py:23
  66.0 10.0 %collective-permute-start.18 = (f32[128,128]{1,0:T(8,128)S(1)}, f32[128,128]{1,0:T(8,128)S(1)}, u32[]{:S(2)}, u32[]{:S(2)}) collective-permute-start(f32[128,128]{1,0:T(8,128)S(1)} %get-tuple-element.52), channel_id=1, source_target_pairs={{0,128},{128,0},{256,384},{384,256},{1,129},{129,1},{257,385},{385... | collective-permute-start | bytes 196616 | tf_op jit(solution)/shard_map/ppermute | solution.py:22
  69.4 10.8 %collective-permute-start.19 = (f32[128,128]{1,0:T(8,128)S(1)}, f32[128,128]{1,0:T(8,128)S(1)}, u32[]{:S(2)}, u32[]{:S(2)}) collective-permute-start(f32[128,128]{1,0:T(8,128)S(1)} %get-tuple-element.53), channel_id=1, source_target_pairs={{128,256},{256,128},{129,257},{257,129},{130,258},{258,130},{131,2... | collective-permute-start | bytes 196616 | tf_op jit(solution)/shard_map/ppermute | solution.py:23
  70.1 10.2 %collective-permute-start.20 = (f32[128,128]{1,0:T(8,128)S(1)}, f32[128,128]{1,0:T(8,128)S(1)}, u32[]{:S(2)}, u32[]{:S(2)}) collective-permute-start(f32[128,128]{1,0:T(8,128)S(1)} %get-tuple-element.50), channel_id=1, source_target_pairs={{0,32},{32,0},{64,96},{96,64},{1,33},{33,1},{65,97},{97,65},{2,34}... | collective-permute-start | bytes 196616 | tf_op jit(solution)/shard_map/ppermute | solution.py:22
  73.5 6.8 %collective-permute-start.21 = (f32[128,128]{1,0:T(8,128)S(1)}, f32[128,128]{1,0:T(8,128)S(1)}, u32[]{:S(2)}, u32[]{:S(2)}) collective-permute-start(f32[128,128]{1,0:T(8,128)S(1)} %get-tuple-element.51), channel_id=1, source_target_pairs={{32,64},{64,32},{33,65},{65,33},{34,66},{66,34},{35,67},{67,35},{3... | collective-permute-start | bytes 196616 | tf_op jit(solution)/shard_map/ppermute | solution.py:23
  74.1 6.2 %collective-permute-start.22 = (f32[128,128]{1,0:T(8,128)S(1)}, f32[128,128]{1,0:T(8,128)S(1)}, u32[]{:S(2)}, u32[]{:S(2)}) collective-permute-start(f32[128,128]{1,0:T(8,128)S(1)} %get-tuple-element.49), channel_id=1, source_target_pairs={{0,1},{1,0},{2,3},{3,2},{4,5},{5,4},{6,7},{7,6},{8,9},{9,8},{10,11... | collective-permute-start | bytes 196616 | tf_op jit(solution)/shard_map/ppermute | solution.py:22
  76.1 6.1 %collective-permute-start.23 = (f32[128,128]{1,0:T(8,128)S(1)}, f32[128,128]{1,0:T(8,128)S(1)}, u32[]{:S(2)}, u32[]{:S(2)}) collective-permute-start(f32[128,128]{1,0:T(8,128)S(1)} %get-tuple-element.48), channel_id=1, source_target_pairs={{1,2},{2,1},{3,4},{4,3},{5,6},{6,5},{7,8},{8,7},{9,10},{10,9},{11,... | collective-permute-start | bytes 196616 | tf_op jit(solution)/shard_map/ppermute | solution.py:23
  83.1 11.6 %collective-permute-start.24 = (f32[128,128]{1,0:T(8,128)S(1)}, f32[128,128]{1,0:T(8,128)S(1)}, u32[]{:S(2)}, u32[]{:S(2)}) collective-permute-start(f32[128,128]{1,0:T(8,128)S(1)} %get-tuple-element.46), channel_id=1, source_target_pairs={{0,128},{128,0},{256,384},{384,256},{1,129},{129,1},{257,385},{385... | collective-permute-start | bytes 196616 | tf_op jit(solution)/shard_map/ppermute | solution.py:22
  87.3 11.7 %collective-permute-start.25 = (f32[128,128]{1,0:T(8,128)S(1)}, f32[128,128]{1,0:T(8,128)S(1)}, u32[]{:S(2)}, u32[]{:S(2)}) collective-permute-start(f32[128,128]{1,0:T(8,128)S(1)} %get-tuple-element.47), channel_id=1, source_target_pairs={{128,256},{256,128},{129,257},{257,129},{130,258},{258,130},{131,2... | collective-permute-start | bytes 196616 | tf_op jit(solution)/shard_map/ppermute | solution.py:23
  87.9 11.0 %collective-permute-start.26 = (f32[128,128]{1,0:T(8,128)S(1)}, f32[128,128]{1,0:T(8,128)S(1)}, u32[]{:S(2)}, u32[]{:S(2)}) collective-permute-start(f32[128,128]{1,0:T(8,128)S(1)} %get-tuple-element.44), channel_id=1, source_target_pairs={{0,32},{32,0},{64,96},{96,64},{1,33},{33,1},{65,97},{97,65},{2,34}... | collective-permute-start | bytes 196616 | tf_op jit(solution)/shard_map/ppermute | solution.py:22
  92.1 6.8 %collective-permute-start.27 = (f32[128,128]{1,0:T(8,128)S(1)}, f32[128,128]{1,0:T(8,128)S(1)}, u32[]{:S(2)}, u32[]{:S(2)}) collective-permute-start(f32[128,128]{1,0:T(8,128)S(1)} %get-tuple-element.45), channel_id=1, source_target_pairs={{32,64},{64,32},{33,65},{65,33},{34,66},{66,34},{35,67},{67,35},{3... | collective-permute-start | bytes 196616 | tf_op jit(solution)/shard_map/ppermute | solution.py:23
  92.8 6.2 %collective-permute-start.28 = (f32[128,128]{1,0:T(8,128)S(1)}, f32[128,128]{1,0:T(8,128)S(1)}, u32[]{:S(2)}, u32[]{:S(2)}) collective-permute-start(f32[128,128]{1,0:T(8,128)S(1)} %get-tuple-element.43), channel_id=1, source_target_pairs={{0,1},{1,0},{2,3},{3,2},{4,5},{5,4},{6,7},{7,6},{8,9},{9,8},{10,11... | collective-permute-start | bytes 196616 | tf_op jit(solution)/shard_map/ppermute | solution.py:22
  94.8 6.1 %collective-permute-start.29 = (f32[128,128]{1,0:T(8,128)S(1)}, f32[128,128]{1,0:T(8,128)S(1)}, u32[]{:S(2)}, u32[]{:S(2)}) collective-permute-start(f32[128,128]{1,0:T(8,128)S(1)} %get-tuple-element.42), channel_id=1, source_target_pairs={{1,2},{2,1},{3,4},{4,3},{5,6},{6,5},{7,8},{8,7},{9,10},{10,9},{11,... | collective-permute-start | bytes 196616 | tf_op jit(solution)/shard_map/ppermute | solution.py:23
  103.1 14.1 %collective-permute-start.30 = (f32[128,128]{1,0:T(8,128)}, f32[128,128]{1,0:T(8,128)S(1)}, u32[]{:S(2)}, u32[]{:S(2)}) collective-permute-start(f32[128,128]{1,0:T(8,128)} %get-tuple-element.40), channel_id=1, source_target_pairs={{0,128},{128,0},{256,384},{384,256},{1,129},{129,1},{257,385},{385... | collective-permute-start | bytes 196616 | tf_op jit(solution)/shard_map/ppermute | solution.py:22
  106.8 15.9 %collective-permute-start.31 = (f32[128,128]{1,0:T(8,128)}, f32[128,128]{1,0:T(8,128)S(1)}, u32[]{:S(2)}, u32[]{:S(2)}) collective-permute-start(f32[128,128]{1,0:T(8,128)} %get-tuple-element.41), channel_id=1, source_target_pairs={{128,256},{256,128},{129,257},{257,129},{130,258},{258,130},{131,2... | collective-permute-start | bytes 196616 | tf_op jit(solution)/shard_map/ppermute | solution.py:23
  110.1 12.7 %collective-permute-start.32 = (f32[128,128]{1,0:T(8,128)}, f32[128,128]{1,0:T(8,128)S(1)}, u32[]{:S(2)}, u32[]{:S(2)}) collective-permute-start(f32[128,128]{1,0:T(8,128)} %get-tuple-element.38), channel_id=1, source_target_pairs={{0,32},{32,0},{64,96},{96,64},{1,33},{33,1},{65,97},{97,65},{2,34}... | collective-permute-start | bytes 196616 | tf_op jit(solution)/shard_map/ppermute | solution.py:22
  114.7 8.1 %collective-permute-start.33 = (f32[128,128]{1,0:T(8,128)}, f32[128,128]{1,0:T(8,128)S(1)}, u32[]{:S(2)}, u32[]{:S(2)}) collective-permute-start(f32[128,128]{1,0:T(8,128)} %get-tuple-element.39), channel_id=1, source_target_pairs={{32,64},{64,32},{33,65},{65,33},{34,66},{66,34},{35,67},{67,35},{3... | collective-permute-start | bytes 196616 | tf_op jit(solution)/shard_map/ppermute | solution.py:23
  115.3 7.5 %collective-permute-start.34 = (f32[128,128]{1,0:T(8,128)}, f32[128,128]{1,0:T(8,128)S(1)}, u32[]{:S(2)}, u32[]{:S(2)}) collective-permute-start(f32[128,128]{1,0:T(8,128)} %get-tuple-element.37), channel_id=1, source_target_pairs={{0,1},{1,0},{2,3},{3,2},{4,5},{5,4},{6,7},{7,6},{8,9},{9,8},{10,11... | collective-permute-start | bytes 196616 | tf_op jit(solution)/shard_map/ppermute | solution.py:22
  117.3 7.4 %collective-permute-start.35 = (f32[128,128]{1,0:T(8,128)S(1)}, f32[128,128]{1,0:T(8,128)S(1)}, u32[]{:S(2)}, u32[]{:S(2)}) collective-permute-start(f32[128,128]{1,0:T(8,128)S(1)} %get-tuple-element.36), channel_id=1, source_target_pairs={{1,2},{2,1},{3,4},{4,3},{5,6},{6,5},{7,8},{8,7},{9,10},{10,9},{11,... | collective-permute-start | bytes 196616 | tf_op jit(solution)/shard_map/ppermute | solution.py:23
  (18 other events, 193.4 us)

commit v2 on v1

--- a/solution.py
+++ b/solution.py
@@ -4,8 +4,10 @@
 from jax.sharding import Mesh
 from jax.sharding import PartitionSpec as P
 
+
 GZ = ("gz_0", "gz_1")
 AXES = (("gx", 0), ("gy", 2), (GZ, 4))
+ROUNDS = ((GZ, 4, 1), ("gx", 0, 0), ("gx", 0, 1), ("gy", 2, 0), ("gy", 2, 1), (GZ, 4, 0))
 MOMENTS = 6
 
 
@@ -14,25 +16,28 @@
 
 
 def from_partners(faces):
-    got = [None] * 6
-    for axis, at in AXES:
-        devices = lax.axis_size(axis)
+    swapped = {}
+    for axis, at, first in ROUNDS:
         odd = lax.axis_index(axis) % 2 == 1
         low, high = faces[at], faces[at + 1]
-        even_pairs = lax.ppermute(jnp.where(odd, low, high), axis, swaps(devices, 0))
-        odd_pairs = lax.ppermute(jnp.where(odd, high, low), axis, swaps(devices, 1))
-        got[at] = jnp.where(odd, even_pairs, odd_pairs)
-        got[at + 1] = jnp.where(odd, odd_pairs, even_pairs)
+        mine = jnp.where(odd, high, low) if first else jnp.where(odd, low, high)
+        swapped[at, first] = lax.ppermute(mine, axis, swaps(lax.axis_size(axis), first))
+    got = []
+    for axis, at in AXES:
+        odd = lax.axis_index(axis) % 2 == 1
+        got.append(jnp.where(odd, swapped[at, 0], swapped[at, 1]))
+        got.append(jnp.where(odd, swapped[at, 1], swapped[at, 0]))
     return jnp.stack(got)
 
 
 def from_everyone(value, axis):
-    copies = jnp.broadcast_to(value, (lax.axis_size(axis), *value.shape))
-    return lax.all_to_all(copies, axis, split_axis=0, concat_axis=0, tiled=True)
+    copies = jnp.broadcast_to(value.reshape(-1), (lax.axis_size(axis), 1, value.size))
+    got = lax.all_to_all(copies, axis, split_axis=0, concat_axis=0, tiled=True)
+    return got.reshape(-1, *value.shape)
 
 
 def totals(moments, scale):
-    for axis in (("gx", "gy"), GZ):
+    for axis in (("gx", "gy", "gz_1"), "gz_0"):
         scale = jnp.broadcast_to(scale, moments.shape[1:])
         packed = jnp.concatenate([moments, scale[None]])
         everyone = from_everyone(packed, axis)
@@ -77,7 +82,7 @@
     weighted_pick = jnp.where(here, weight, 0.0).astype(jnp.bfloat16)
 
     def minus_partner(own):
-        faces = own.reshape(6, face_len, loads)
+        faces = own.astype(jnp.bfloat16).reshape(6, face_len, loads)
         partners = from_partners(faces)
         return (faces.astype(jnp.float32) - partners.astype(jnp.float32)).reshape(slots, loads)
 
@@ -96,15 +101,14 @@
     def dots(left, right):
         return jnp.sum(left * right, axis=0)
 
-    def largest_diagonal(op):
-        on = jnp.arange(width).reshape(width, 1) == columns
-        return jnp.max(jnp.where(on, op, 0).astype(jnp.float32))
+    def size_of(op):
+        return jnp.max(jnp.abs(op[:8, :128].astype(jnp.float32)))
 
     picked = jnp.dot(pick, displaced, preferred_element_type=jnp.float32).astype(jnp.bfloat16)
     residual = minus_partner(picked)
     schur_slots = on_slots(weighted_pick, schur_op)
     flex_slots = on_slots(pick, flex_op)
-    scale = largest_diagonal(flex_op) * largest_diagonal(schur_op)
+    scale = size_of(flex_op) * size_of(schur_op)
     down = 1.0 / scale
 
     smooth0 = apply(schur_slots, residual)

time: 179 us -> 175 us (0.978)
  blocking collectives: 50.6 us -> 45.3 us
  waiting for transfers between devices: 13.4 us -> 10.1 us
  other arithmetic: 5.71 us -> 8.96 us
    all_to_all x2, blocking collectives: 50.6 us -> 45.3 us  [from_everyone(): got = lax.all_to_all(copies, axis, split_axis=0, concat_axis=0, tiled=True)]
    ppermute x36, waiting for transfers between devices: 13.4 us -> 10.1 us  [from_partners(): lax.ppermute(mine, axis, swaps(lax.axis_size(axis), first))]
  transfers between devices with their start and end apart: 36 -> 36, of which waited for: 6 -> 5; matrix products, arithmetic and copies ran while one was open for 4% -> 5% of each run, Pallas kernels for 0% -> 0%
where the time goes in v2:
time: 175 us; the launch traced here: 173 us
  starting transfers between devices  96 us (55%)
  blocking collectives  45.3 us (26%)
  waiting for transfers between devices  10.1 us (6%)
  matrix products  9.01 us (5%)
  other arithmetic  8.96 us (5%)
  between operations  2.4 us (1%)
    ppermute x36, starting transfers between devices, from_partners(): lax.ppermute(mine, axis, swaps(lax.axis_size(axis), first))  96 us
    all_to_all x2, blocking collectives, from_everyone(): got = lax.all_to_all(copies, axis, split_axis=0, concat_axis=0, tiled=True)  45.3 us
    ppermute x36, waiting for transfers between devices, from_partners(): lax.ppermute(mine, axis, swaps(lax.axis_size(axis), first))  10.1 us
    dot_general x2, matrix products, on_slots(): lax.dot_general(half, table, (((1,), (1,)), ((), ())), preferred_element_...  5.61 us
  transfers between devices with their start and end apart: 36, of which 5 were waited for; matrix products, arithmetic and copies ran while one was open for 5% of the time, Pallas kernels for 0%

profile of v2, /device:TPU:1, one launch (start us, length us, event | category | flops | bytes accessed | tf_op | source)
XLA Modules:
  0.0 173.4 jit_solution(11750754036484521979)
XLA Ops:
  1.5 3.9 %collective-permute-start = (bf16[128,128]{1,0:T(8,128)(2,1)S(1)}, bf16[128,128]{1,0:T(8,128)(2,1)S(1)}, u32[]{:S(2)}, u32[]{:S(2)}) collective-permute-start(bf16[128,128]{1,0:T(8,128)(2,1)S(1)} %get-tuple-element.73), channel_id=1, source_target_pairs={{0,128},{128,0},{256,384},{384,256},{1,129},{129,1},{257,385},{385... | collective-permute-start | bytes 98312 | tf_op jit(solution)/shard_map/ppermute | solution.py:24
  6.2 3.2 %collective-permute-start.2 = (bf16[128,128]{1,0:T(8,128)(2,1)S(1)}, bf16[128,128]{1,0:T(8,128)(2,1)S(1)}, u32[]{:S(2)}, u32[]{:S(2)}) collective-permute-start(bf16[128,128]{1,0:T(8,128)(2,1)S(1)} %get-tuple-element.71), channel_id=1, source_target_pairs={{0,32},{32,0},{64,96},{96,64},{1,33},{33,1},{65,97},{97,65},{2,34}... | collective-permute-start | bytes 98312 | tf_op jit(solution)/shard_map/ppermute | solution.py:24
  10.0 5.4 %collective-permute-start.4 = (bf16[128,128]{1,0:T(8,128)(2,1)S(1)}, bf16[128,128]{1,0:T(8,128)(2,1)S(1)}, u32[]{:S(2)}, u32[]{:S(2)}) collective-permute-start(bf16[128,128]{1,0:T(8,128)(2,1)S(1)} %get-tuple-element.75), channel_id=1, source_target_pairs={{0,1},{1,0},{2,3},{3,2},{4,5},{5,4},{6,7},{7,6},{8,9},{9,8},{10,11... | collective-permute-start | bytes 98312 | tf_op jit(solution)/shard_map/ppermute | solution.py:24
  15.5 2.2 %convolution_convert_fusion = bf16[768,768]{1,0:T(8,128)(2,1)S(1)} fusion(bf16[768]{0:T(1024)(128)(2,1)S(1)} %divide_reduce_fusion, s32[768]{0:T(1024)S(1)} %reduce.4, bf16[1,1,1,768,768]{4,3,2,1,0:T(8,128)(2,1)S(1)} %copy-done.15), kind=kOutput, calls=%fused_computation.7 | convolution fusion | flops 1815478272 | bytes 2363904 | tf_op jit(solution)/shard_map/dot_general | solution.py:91
  17.7 1.9 %collective-permute-start.5 = (bf16[128,128]{1,0:T(8,128)(2,1)S(1)}, bf16[128,128]{1,0:T(8,128)(2,1)S(1)}, u32[]{:S(2)}, u32[]{:S(2)}) collective-permute-start(bf16[128,128]{1,0:T(8,128)(2,1)S(1)} %get-tuple-element.70), channel_id=1, source_target_pairs={{1,2},{2,1},{3,4},{4,3},{5,6},{6,5},{7,8},{8,7},{9,10},{10,9},{11,... | collective-permute-start | bytes 98312 | tf_op jit(solution)/shard_map/ppermute | solution.py:24
  19.8 3.2 %collective-permute-done.5 = bf16[128,128]{1,0:T(8,128)(2,1)S(1)} collective-permute-done((bf16[128,128]{1,0:T(8,128)(2,1)S(1)}, bf16[128,128]{1,0:T(8,128)(2,1)S(1)}, u32[]{:S(2)}, u32[]{:S(2)}) %collective-permute-start.5) | collective-permute-done | bytes 32800 | tf_op jit(solution)/shard_map/ppermute | solution.py:24
  23.8 4.9 %collective-permute-start.6 = (bf16[128,128]{1,0:T(8,128)(2,1)S(1)}, bf16[128,128]{1,0:T(8,128)(2,1)S(1)}, u32[]{:S(2)}, u32[]{:S(2)}) collective-permute-start(bf16[128,128]{1,0:T(8,128)(2,1)S(1)} %get-tuple-element.67), channel_id=1, source_target_pairs={{0,128},{128,0},{256,384},{384,256},{1,129},{129,1},{257,385},{385... | collective-permute-start | bytes 98312 | tf_op jit(solution)/shard_map/ppermute | solution.py:24
  29.4 3.4 %fusion.4 = bf16[768,768]{1,0:T(8,128)(2,1)S(1)} fusion(s32[768]{0:T(1024)S(1)} %reduce.4, bf16[1,1,1,768,768]{4,3,2,1,0:T(8,128)(2,1)} %param.6), kind=kOutput, calls=%fused_computation.6 | convolution fusion | flops 1814298624 | bytes 2362368 | tf_op jit(solution)/shard_map/dot_general | solution.py:91
  32.8 4.9 %collective-permute-start.8 = (bf16[128,128]{1,0:T(8,128)(2,1)S(1)}, bf16[128,128]{1,0:T(8,128)(2,1)S(1)}, u32[]{:S(2)}, u32[]{:S(2)}) collective-permute-start(bf16[128,128]{1,0:T(8,128)(2,1)S(1)} %get-tuple-element.65), channel_id=1, source_target_pairs={{0,32},{32,0},{64,96},{96,64},{1,33},{33,1},{65,97},{97,65},{2,34}... | collective-permute-start | bytes 98312 | tf_op jit(solution)/shard_map/ppermute | solution.py:24
  38.4 1.9 %collective-permute-start.10 = (bf16[128,128]{1,0:T(8,128)(2,1)S(1)}, bf16[128,128]{1,0:T(8,128)(2,1)S(1)}, u32[]{:S(2)}, u32[]{:S(2)}) collective-permute-start(bf16[128,128]{1,0:T(8,128)(2,1)S(1)} %get-tuple-element.69), channel_id=1, source_target_pairs={{0,1},{1,0},{2,3},{3,2},{4,5},{5,4},{6,7},{7,6},{8,9},{9,8},{10,11... | collective-permute-start | bytes 98312 | tf_op jit(solution)/shard_map/ppermute | solution.py:24
  40.3 3.2 %collective-permute-start.11 = (bf16[128,128]{1,0:T(8,128)(2,1)S(1)}, bf16[128,128]{1,0:T(8,128)(2,1)S(1)}, u32[]{:S(2)}, u32[]{:S(2)}) collective-permute-start(bf16[128,128]{1,0:T(8,128)(2,1)S(1)} %get-tuple-element.64), channel_id=1, source_target_pairs={{1,2},{2,1},{3,4},{4,3},{5,6},{6,5},{7,8},{8,7},{9,10},{10,9},{11,... | collective-permute-start | bytes 98312 | tf_op jit(solution)/shard_map/ppermute | solution.py:24
  43.7 1.9 %collective-permute-done.11 = bf16[128,128]{1,0:T(8,128)(2,1)S(1)} collective-permute-done((bf16[128,128]{1,0:T(8,128)(2,1)S(1)}, bf16[128,128]{1,0:T(8,128)(2,1)S(1)}, u32[]{:S(2)}, u32[]{:S(2)}) %collective-permute-start.11) | collective-permute-done | bytes 32800 | tf_op jit(solution)/shard_map/ppermute | solution.py:24
  46.4 5.0 %collective-permute-start.12 = (bf16[128,128]{1,0:T(8,128)(2,1)S(1)}, bf16[128,128]{1,0:T(8,128)(2,1)S(1)}, u32[]{:S(2)}, u32[]{:S(2)}) collective-permute-start(bf16[128,128]{1,0:T(8,128)(2,1)S(1)} %get-tuple-element.61), channel_id=1, source_target_pairs={{0,128},{128,0},{256,384},{384,256},{1,129},{129,1},{257,385},{385... | collective-permute-start | bytes 98312 | tf_op jit(solution)/shard_map/ppermute | solution.py:24
  52.1 4.9 %collective-permute-start.14 = (bf16[128,128]{1,0:T(8,128)(2,1)S(1)}, bf16[128,128]{1,0:T(8,128)(2,1)S(1)}, u32[]{:S(2)}, u32[]{:S(2)}) collective-permute-start(bf16[128,128]{1,0:T(8,128)(2,1)S(1)} %get-tuple-element.59), channel_id=1, source_target_pairs={{0,32},{32,0},{64,96},{96,64},{1,33},{33,1},{65,97},{97,65},{2,34}... | collective-permute-start | bytes 98312 | tf_op jit(solution)/shard_map/ppermute | solution.py:24
  57.6 1.9 %collective-permute-start.16 = (bf16[128,128]{1,0:T(8,128)(2,1)S(1)}, bf16[128,128]{1,0:T(8,128)(2,1)S(1)}, u32[]{:S(2)}, u32[]{:S(2)}) collective-permute-start(bf16[128,128]{1,0:T(8,128)(2,1)S(1)} %get-tuple-element.63), channel_id=1, source_target_pairs={{0,1},{1,0},{2,3},{3,2},{4,5},{5,4},{6,7},{7,6},{8,9},{9,8},{10,11... | collective-permute-start | bytes 98312 | tf_op jit(solution)/shard_map/ppermute | solution.py:24
  59.6 3.0 %collective-permute-start.17 = (bf16[128,128]{1,0:T(8,128)(2,1)S(1)}, bf16[128,128]{1,0:T(8,128)(2,1)S(1)}, u32[]{:S(2)}, u32[]{:S(2)}) collective-permute-start(bf16[128,128]{1,0:T(8,128)(2,1)S(1)} %get-tuple-element.58), channel_id=1, source_target_pairs={{1,2},{2,1},{3,4},{4,3},{5,6},{6,5},{7,8},{8,7},{9,10},{10,9},{11,... | collective-permute-start | bytes 98312 | tf_op jit(solution)/shard_map/ppermute | solution.py:24
  62.8 2.0 %collective-permute-done.17 = bf16[128,128]{1,0:T(8,128)(2,1)S(1)} collective-permute-done((bf16[128,128]{1,0:T(8,128)(2,1)S(1)}, bf16[128,128]{1,0:T(8,128)(2,1)S(1)}, u32[]{:S(2)}, u32[]{:S(2)}) %collective-permute-start.17) | collective-permute-done | bytes 32800 | tf_op jit(solution)/shard_map/ppermute | solution.py:24
  65.6 3.5 %collective-permute-start.18 = (bf16[128,128]{1,0:T(8,128)(2,1)S(1)}, bf16[128,128]{1,0:T(8,128)(2,1)S(1)}, u32[]{:S(2)}, u32[]{:S(2)}) collective-permute-start(bf16[128,128]{1,0:T(8,128)(2,1)S(1)} %get-tuple-element.55), channel_id=1, source_target_pairs={{0,128},{128,0},{256,384},{384,256},{1,129},{129,1},{257,385},{385... | collective-permute-start | bytes 98312 | tf_op jit(solution)/shard_map/ppermute | solution.py:24
  69.7 3.4 %collective-permute-start.20 = (bf16[128,128]{1,0:T(8,128)(2,1)S(1)}, bf16[128,128]{1,0:T(8,128)(2,1)S(1)}, u32[]{:S(2)}, u32[]{:S(2)}) collective-permute-start(bf16[128,128]{1,0:T(8,128)(2,1)S(1)} %get-tuple-element.53), channel_id=1, source_target_pairs={{0,32},{32,0},{64,96},{96,64},{1,33},{33,1},{65,97},{97,65},{2,34}... | collective-permute-start | bytes 98312 | tf_op jit(solution)/shard_map/ppermute | solution.py:24
  73.8 1.9 %collective-permute-start.22 = (bf16[128,128]{1,0:T(8,128)(2,1)S(1)}, bf16[128,128]{1,0:T(8,128)(2,1)S(1)}, u32[]{:S(2)}, u32[]{:S(2)}) collective-permute-start(bf16[128,128]{1,0:T(8,128)(2,1)S(1)} %get-tuple-element.57), channel_id=1, source_target_pairs={{0,1},{1,0},{2,3},{3,2},{4,5},{5,4},{6,7},{7,6},{8,9},{9,8},{10,11... | collective-permute-start | bytes 98312 | tf_op jit(solution)/shard_map/ppermute | solution.py:24
  75.7 4.2 %collective-permute-start.23 = (bf16[128,128]{1,0:T(8,128)(2,1)S(1)}, bf16[128,128]{1,0:T(8,128)(2,1)S(1)}, u32[]{:S(2)}, u32[]{:S(2)}) collective-permute-start(bf16[128,128]{1,0:T(8,128)(2,1)S(1)} %get-tuple-element.52), channel_id=1, source_target_pairs={{1,2},{2,1},{3,4},{4,3},{5,6},{6,5},{7,8},{8,7},{9,10},{10,9},{11,... | collective-permute-start | bytes 98312 | tf_op jit(solution)/shard_map/ppermute | solution.py:24
  80.0 1.4 collective-permute-done.23
  82.3 4.2 %collective-permute-start.24 = (bf16[128,128]{1,0:T(8,128)(2,1)S(1)}, bf16[128,128]{1,0:T(8,128)(2,1)S(1)}, u32[]{:S(2)}, u32[]{:S(2)}) collective-permute-start(bf16[128,128]{1,0:T(8,128)(2,1)S(1)} %get-tuple-element.49), channel_id=1, source_target_pairs={{0,128},{128,0},{256,384},{384,256},{1,129},{129,1},{257,385},{385... | collective-permute-start | bytes 98312 | tf_op jit(solution)/shard_map/ppermute | solution.py:24
  87.1 4.2 %collective-permute-start.26 = (bf16[128,128]{1,0:T(8,128)(2,1)S(1)}, bf16[128,128]{1,0:T(8,128)(2,1)S(1)}, u32[]{:S(2)}, u32[]{:S(2)}) collective-permute-start(bf16[128,128]{1,0:T(8,128)(2,1)S(1)} %get-tuple-element.47), channel_id=1, source_target_pairs={{0,32},{32,0},{64,96},{96,64},{1,33},{33,1},{65,97},{97,65},{2,34}... | collective-permute-start | bytes 98312 | tf_op jit(solution)/shard_map/ppermute | solution.py:24
  92.0 1.9 %collective-permute-start.28 = (bf16[128,128]{1,0:T(8,128)(2,1)S(1)}, bf16[128,128]{1,0:T(8,128)(2,1)S(1)}, u32[]{:S(2)}, u32[]{:S(2)}) collective-permute-start(bf16[128,128]{1,0:T(8,128)(2,1)S(1)} %get-tuple-element.51), channel_id=1, source_target_pairs={{0,1},{1,0},{2,3},{3,2},{4,5},{5,4},{6,7},{7,6},{8,9},{9,8},{10,11... | collective-permute-start | bytes 98312 | tf_op jit(solution)/shard_map/ppermute | solution.py:24
  93.9 4.2 %collective-permute-start.29 = (bf16[128,128]{1,0:T(8,128)(2,1)S(1)}, bf16[128,128]{1,0:T(8,128)(2,1)S(1)}, u32[]{:S(2)}, u32[]{:S(2)}) collective-permute-start(bf16[128,128]{1,0:T(8,128)(2,1)S(1)} %get-tuple-element.46), channel_id=1, source_target_pairs={{1,2},{2,1},{3,4},{4,3},{5,6},{6,5},{7,8},{8,7},{9,10},{10,9},{11,... | collective-permute-start | bytes 98312 | tf_op jit(solution)/shard_map/ppermute | solution.py:24
  101.0 3.7 %collective-permute-start.30 = (bf16[128,128]{1,0:T(8,128)(2,1)}, bf16[128,128]{1,0:T(8,128)(2,1)}, u32[]{:S(2)}, u32[]{:S(2)}) collective-permute-start(bf16[128,128]{1,0:T(8,128)(2,1)} %get-tuple-element.43), channel_id=1, source_target_pairs={{0,128},{128,0},{256,384},{384,256},{1,129},{129,1},{257,385},{385... | collective-permute-start | bytes 98312 | tf_op jit(solution)/shard_map/ppermute | solution.py:24
  108.7 4.6 %collective-permute-start.32 = (bf16[128,128]{1,0:T(8,128)(2,1)}, bf16[128,128]{1,0:T(8,128)(2,1)S(1)}, u32[]{:S(2)}, u32[]{:S(2)}) collective-permute-start(bf16[128,128]{1,0:T(8,128)(2,1)} %get-tuple-element.41), channel_id=1, source_target_pairs={{0,32},{32,0},{64,96},{96,64},{1,33},{33,1},{65,97},{97,65},{2,34}... | collective-permute-start | bytes 98312 | tf_op jit(solution)/shard_map/ppermute | solution.py:24
  113.9 1.9 %collective-permute-start.34 = (bf16[128,128]{1,0:T(8,128)(2,1)}, bf16[128,128]{1,0:T(8,128)(2,1)S(1)}, u32[]{:S(2)}, u32[]{:S(2)}) collective-permute-start(bf16[128,128]{1,0:T(8,128)(2,1)} %get-tuple-element.45), channel_id=1, source_target_pairs={{0,1},{1,0},{2,3},{3,2},{4,5},{5,4},{6,7},{7,6},{8,9},{9,8},{10,11... | collective-permute-start | bytes 98312 | tf_op jit(solution)/shard_map/ppermute | solution.py:24
  115.9 5.6 %collective-permute-start.35 = (bf16[128,128]{1,0:T(8,128)(2,1)}, bf16[128,128]{1,0:T(8,128)(2,1)S(1)}, u32[]{:S(2)}, u32[]{:S(2)}) collective-permute-start(bf16[128,128]{1,0:T(8,128)(2,1)} %get-tuple-element.40), channel_id=1, source_target_pairs={{1,2},{2,1},{3,4},{4,3},{5,6},{6,5},{7,8},{8,7},{9,10},{10,9},{11,... | collective-permute-start | bytes 98312 | tf_op jit(solution)/shard_map/ppermute | solution.py:24
  126.2 14.4 %all_to_all.10 = f32[32,1,896]{2,1,0:T(1,128)S(1)} all-to-all(f32[32,1,896]{2,1,0:T(1,128)S(1)} %broadcast_in_dim.31), channel_id=1, replica_groups=mesh['gx'=4,'gy'=4,'gz_0'=16,'gz_1'=2] {'gx','gy','gz_1'}, dimensions={0} | all-to-all | bytes 229376 | tf_op jit(solution)/shard_map/all_to_all | solution.py:35
  141.1 30.9 %all_to_all.11 = f32[16,1,896]{2,1,0:T(1,128)S(1)} all-to-all(f32[16,1,896]{2,1,0:T(1,128)S(1)} %broadcast_in_dim.33), channel_id=1, replica_groups=mesh['gx'=4,'gy'=4,'gz_0'=16,'gz_1'=2] {'gz_0'}, dimensions={0} | all-to-all | bytes 114688 | tf_op jit(solution)/shard_map/all_to_all | solution.py:35
  (158 shorter events, 24.1 us)
Async XLA Ops:
  1.5 16.2 %collective-permute-start = (bf16[128,128]{1,0:T(8,128)(2,1)S(1)}, bf16[128,128]{1,0:T(8,128)(2,1)S(1)}, u32[]{:S(2)}, u32[]{:S(2)}) collective-permute-start(bf16[128,128]{1,0:T(8,128)(2,1)S(1)} %get-tuple-element.73), channel_id=1, source_target_pairs={{0,128},{128,0},{256,384},{384,256},{1,129},{129,1},{257,385},{385... | collective-permute-start | bytes 98312 | tf_op jit(solution)/shard_map/ppermute | solution.py:24
  5.5 14.2 %collective-permute-start.1 = (bf16[128,128]{1,0:T(8,128)(2,1)S(1)}, bf16[128,128]{1,0:T(8,128)(2,1)S(1)}, u32[]{:S(2)}, u32[]{:S(2)}) collective-permute-start(bf16[128,128]{1,0:T(8,128)(2,1)S(1)} %get-tuple-element.74), channel_id=1, source_target_pairs={{128,256},{256,128},{129,257},{257,129},{130,258},{258,130},{131,2... | collective-permute-start | bytes 98312 | tf_op jit(solution)/shard_map/ppermute | solution.py:24
  6.2 13.6 %collective-permute-start.2 = (bf16[128,128]{1,0:T(8,128)(2,1)S(1)}, bf16[128,128]{1,0:T(8,128)(2,1)S(1)}, u32[]{:S(2)}, u32[]{:S(2)}) collective-permute-start(bf16[128,128]{1,0:T(8,128)(2,1)S(1)} %get-tuple-element.71), channel_id=1, source_target_pairs={{0,32},{32,0},{64,96},{96,64},{1,33},{33,1},{65,97},{97,65},{2,34}... | collective-permute-start | bytes 98312 | tf_op jit(solution)/shard_map/ppermute | solution.py:24
  9.4 10.4 %collective-permute-start.3 = (bf16[128,128]{1,0:T(8,128)(2,1)S(1)}, bf16[128,128]{1,0:T(8,128)(2,1)S(1)}, u32[]{:S(2)}, u32[]{:S(2)}) collective-permute-start(bf16[128,128]{1,0:T(8,128)(2,1)S(1)} %get-tuple-element.72), channel_id=1, source_target_pairs={{32,64},{64,32},{33,65},{65,33},{34,66},{66,34},{35,67},{67,35},{3... | collective-permute-start | bytes 98312 | tf_op jit(solution)/shard_map/ppermute | solution.py:24
  10.0 9.7 %collective-permute-start.4 = (bf16[128,128]{1,0:T(8,128)(2,1)S(1)}, bf16[128,128]{1,0:T(8,128)(2,1)S(1)}, u32[]{:S(2)}, u32[]{:S(2)}) collective-permute-start(bf16[128,128]{1,0:T(8,128)(2,1)S(1)} %get-tuple-element.75), channel_id=1, source_target_pairs={{0,1},{1,0},{2,3},{3,2},{4,5},{5,4},{6,7},{7,6},{8,9},{9,8},{10,11... | collective-permute-start | bytes 98312 | tf_op jit(solution)/shard_map/ppermute | solution.py:24
  23.8 16.5 %collective-permute-start.6 = (bf16[128,128]{1,0:T(8,128)(2,1)S(1)}, bf16[128,128]{1,0:T(8,128)(2,1)S(1)}, u32[]{:S(2)}, u32[]{:S(2)}) collective-permute-start(bf16[128,128]{1,0:T(8,128)(2,1)S(1)} %get-tuple-element.67), channel_id=1, source_target_pairs={{0,128},{128,0},{256,384},{384,256},{1,129},{129,1},{257,385},{385... | collective-permute-start | bytes 98312 | tf_op jit(solution)/shard_map/ppermute | solution.py:24
  28.7 14.9 %collective-permute-start.7 = (bf16[128,128]{1,0:T(8,128)(2,1)S(1)}, bf16[128,128]{1,0:T(8,128)(2,1)S(1)}, u32[]{:S(2)}, u32[]{:S(2)}) collective-permute-start(bf16[128,128]{1,0:T(8,128)(2,1)S(1)} %get-tuple-element.68), channel_id=1, source_target_pairs={{128,256},{256,128},{129,257},{257,129},{130,258},{258,130},{131,2... | collective-permute-start | bytes 98312 | tf_op jit(solution)/shard_map/ppermute | solution.py:24
  32.8 10.8 %collective-permute-start.8 = (bf16[128,128]{1,0:T(8,128)(2,1)S(1)}, bf16[128,128]{1,0:T(8,128)(2,1)S(1)}, u32[]{:S(2)}, u32[]{:S(2)}) collective-permute-start(bf16[128,128]{1,0:T(8,128)(2,1)S(1)} %get-tuple-element.65), channel_id=1, source_target_pairs={{0,32},{32,0},{64,96},{96,64},{1,33},{33,1},{65,97},{97,65},{2,34}... | collective-permute-start | bytes 98312 | tf_op jit(solution)/shard_map/ppermute | solution.py:24
  37.7 5.9 %collective-permute-start.9 = (bf16[128,128]{1,0:T(8,128)(2,1)S(1)}, bf16[128,128]{1,0:T(8,128)(2,1)S(1)}, u32[]{:S(2)}, u32[]{:S(2)}) collective-permute-start(bf16[128,128]{1,0:T(8,128)(2,1)S(1)} %get-tuple-element.66), channel_id=1, source_target_pairs={{32,64},{64,32},{33,65},{65,33},{34,66},{66,34},{35,67},{67,35},{3... | collective-permute-start | bytes 98312 | tf_op jit(solution)/shard_map/ppermute | solution.py:24
  38.4 5.3 %collective-permute-start.10 = (bf16[128,128]{1,0:T(8,128)(2,1)S(1)}, bf16[128,128]{1,0:T(8,128)(2,1)S(1)}, u32[]{:S(2)}, u32[]{:S(2)}) collective-permute-start(bf16[128,128]{1,0:T(8,128)(2,1)S(1)} %get-tuple-element.69), channel_id=1, source_target_pairs={{0,1},{1,0},{2,3},{3,2},{4,5},{5,4},{6,7},{7,6},{8,9},{9,8},{10,11... | collective-permute-start | bytes 98312 | tf_op jit(solution)/shard_map/ppermute | solution.py:24
  46.4 13.2 %collective-permute-start.12 = (bf16[128,128]{1,0:T(8,128)(2,1)S(1)}, bf16[128,128]{1,0:T(8,128)(2,1)S(1)}, u32[]{:S(2)}, u32[]{:S(2)}) collective-permute-start(bf16[128,128]{1,0:T(8,128)(2,1)S(1)} %get-tuple-element.61), channel_id=1, source_target_pairs={{0,128},{128,0},{256,384},{384,256},{1,129},{129,1},{257,385},{385... | collective-permute-start | bytes 98312 | tf_op jit(solution)/shard_map/ppermute | solution.py:24
  51.4 11.2 %collective-permute-start.13 = (bf16[128,128]{1,0:T(8,128)(2,1)S(1)}, bf16[128,128]{1,0:T(8,128)(2,1)S(1)}, u32[]{:S(2)}, u32[]{:S(2)}) collective-permute-start(bf16[128,128]{1,0:T(8,128)(2,1)S(1)} %get-tuple-element.62), channel_id=1, source_target_pairs={{128,256},{256,128},{129,257},{257,129},{130,258},{258,130},{131,2... | collective-permute-start | bytes 98312 | tf_op jit(solution)/shard_map/ppermute | solution.py:24
  52.1 10.6 %collective-permute-start.14 = (bf16[128,128]{1,0:T(8,128)(2,1)S(1)}, bf16[128,128]{1,0:T(8,128)(2,1)S(1)}, u32[]{:S(2)}, u32[]{:S(2)}) collective-permute-start(bf16[128,128]{1,0:T(8,128)(2,1)S(1)} %get-tuple-element.59), channel_id=1, source_target_pairs={{0,32},{32,0},{64,96},{96,64},{1,33},{33,1},{65,97},{97,65},{2,34}... | collective-permute-start | bytes 98312 | tf_op jit(solution)/shard_map/ppermute | solution.py:24
  57.0 5.7 %collective-permute-start.15 = (bf16[128,128]{1,0:T(8,128)(2,1)S(1)}, bf16[128,128]{1,0:T(8,128)(2,1)S(1)}, u32[]{:S(2)}, u32[]{:S(2)}) collective-permute-start(bf16[128,128]{1,0:T(8,128)(2,1)S(1)} %get-tuple-element.60), channel_id=1, source_target_pairs={{32,64},{64,32},{33,65},{65,33},{34,66},{66,34},{35,67},{67,35},{3... | collective-permute-start | bytes 98312 | tf_op jit(solution)/shard_map/ppermute | solution.py:24
  65.6 10.1 %collective-permute-start.18 = (bf16[128,128]{1,0:T(8,128)(2,1)S(1)}, bf16[128,128]{1,0:T(8,128)(2,1)S(1)}, u32[]{:S(2)}, u32[]{:S(2)}) collective-permute-start(bf16[128,128]{1,0:T(8,128)(2,1)S(1)} %get-tuple-element.55), channel_id=1, source_target_pairs={{0,128},{128,0},{256,384},{384,256},{1,129},{129,1},{257,385},{385... | collective-permute-start | bytes 98312 | tf_op jit(solution)/shard_map/ppermute | solution.py:24
  69.1 10.8 %collective-permute-start.19 = (bf16[128,128]{1,0:T(8,128)(2,1)S(1)}, bf16[128,128]{1,0:T(8,128)(2,1)S(1)}, u32[]{:S(2)}, u32[]{:S(2)}) collective-permute-start(bf16[128,128]{1,0:T(8,128)(2,1)S(1)} %get-tuple-element.56), channel_id=1, source_target_pairs={{128,256},{256,128},{129,257},{257,129},{130,258},{258,130},{131,2... | collective-permute-start | bytes 98312 | tf_op jit(solution)/shard_map/ppermute | solution.py:24
  69.7 10.2 %collective-permute-start.20 = (bf16[128,128]{1,0:T(8,128)(2,1)S(1)}, bf16[128,128]{1,0:T(8,128)(2,1)S(1)}, u32[]{:S(2)}, u32[]{:S(2)}) collective-permute-start(bf16[128,128]{1,0:T(8,128)(2,1)S(1)} %get-tuple-element.53), channel_id=1, source_target_pairs={{0,32},{32,0},{64,96},{96,64},{1,33},{33,1},{65,97},{97,65},{2,34}... | collective-permute-start | bytes 98312 | tf_op jit(solution)/shard_map/ppermute | solution.py:24
  73.1 6.8 %collective-permute-start.21 = (bf16[128,128]{1,0:T(8,128)(2,1)S(1)}, bf16[128,128]{1,0:T(8,128)(2,1)S(1)}, u32[]{:S(2)}, u32[]{:S(2)}) collective-permute-start(bf16[128,128]{1,0:T(8,128)(2,1)S(1)} %get-tuple-element.54), channel_id=1, source_target_pairs={{32,64},{64,32},{33,65},{65,33},{34,66},{66,34},{35,67},{67,35},{3... | collective-permute-start | bytes 98312 | tf_op jit(solution)/shard_map/ppermute | solution.py:24
  73.8 6.2 %collective-permute-start.22 = (bf16[128,128]{1,0:T(8,128)(2,1)S(1)}, bf16[128,128]{1,0:T(8,128)(2,1)S(1)}, u32[]{:S(2)}, u32[]{:S(2)}) collective-permute-start(bf16[128,128]{1,0:T(8,128)(2,1)S(1)} %get-tuple-element.57), channel_id=1, source_target_pairs={{0,1},{1,0},{2,3},{3,2},{4,5},{5,4},{6,7},{7,6},{8,9},{9,8},{10,11... | collective-permute-start | bytes 98312 | tf_op jit(solution)/shard_map/ppermute | solution.py:24
  75.7 5.8 %collective-permute-start.23 = (bf16[128,128]{1,0:T(8,128)(2,1)S(1)}, bf16[128,128]{1,0:T(8,128)(2,1)S(1)}, u32[]{:S(2)}, u32[]{:S(2)}) collective-permute-start(bf16[128,128]{1,0:T(8,128)(2,1)S(1)} %get-tuple-element.52), channel_id=1, source_target_pairs={{1,2},{2,1},{3,4},{4,3},{5,6},{6,5},{7,8},{8,7},{9,10},{10,9},{11,... | collective-permute-start | bytes 98312 | tf_op jit(solution)/shard_map/ppermute | solution.py:24
  82.3 11.6 %collective-permute-start.24 = (bf16[128,128]{1,0:T(8,128)(2,1)S(1)}, bf16[128,128]{1,0:T(8,128)(2,1)S(1)}, u32[]{:S(2)}, u32[]{:S(2)}) collective-permute-start(bf16[128,128]{1,0:T(8,128)(2,1)S(1)} %get-tuple-element.49), channel_id=1, source_target_pairs={{0,128},{128,0},{256,384},{384,256},{1,129},{129,1},{257,385},{385... | collective-permute-start | bytes 98312 | tf_op jit(solution)/shard_map/ppermute | solution.py:24
  86.4 11.7 %collective-permute-start.25 = (bf16[128,128]{1,0:T(8,128)(2,1)S(1)}, bf16[128,128]{1,0:T(8,128)(2,1)S(1)}, u32[]{:S(2)}, u32[]{:S(2)}) collective-permute-start(bf16[128,128]{1,0:T(8,128)(2,1)S(1)} %get-tuple-element.50), channel_id=1, source_target_pairs={{128,256},{256,128},{129,257},{257,129},{130,258},{258,130},{131,2... | collective-permute-start | bytes 98312 | tf_op jit(solution)/shard_map/ppermute | solution.py:24
  87.1 11.0 %collective-permute-start.26 = (bf16[128,128]{1,0:T(8,128)(2,1)S(1)}, bf16[128,128]{1,0:T(8,128)(2,1)S(1)}, u32[]{:S(2)}, u32[]{:S(2)}) collective-permute-start(bf16[128,128]{1,0:T(8,128)(2,1)S(1)} %get-tuple-element.47), channel_id=1, source_target_pairs={{0,32},{32,0},{64,96},{96,64},{1,33},{33,1},{65,97},{97,65},{2,34}... | collective-permute-start | bytes 98312 | tf_op jit(solution)/shard_map/ppermute | solution.py:24
  91.3 6.8 %collective-permute-start.27 = (bf16[128,128]{1,0:T(8,128)(2,1)S(1)}, bf16[128,128]{1,0:T(8,128)(2,1)S(1)}, u32[]{:S(2)}, u32[]{:S(2)}) collective-permute-start(bf16[128,128]{1,0:T(8,128)(2,1)S(1)} %get-tuple-element.48), channel_id=1, source_target_pairs={{32,64},{64,32},{33,65},{65,33},{34,66},{66,34},{35,67},{67,35},{3... | collective-permute-start | bytes 98312 | tf_op jit(solution)/shard_map/ppermute | solution.py:24
  92.0 6.2 %collective-permute-start.28 = (bf16[128,128]{1,0:T(8,128)(2,1)S(1)}, bf16[128,128]{1,0:T(8,128)(2,1)S(1)}, u32[]{:S(2)}, u32[]{:S(2)}) collective-permute-start(bf16[128,128]{1,0:T(8,128)(2,1)S(1)} %get-tuple-element.51), channel_id=1, source_target_pairs={{0,1},{1,0},{2,3},{3,2},{4,5},{5,4},{6,7},{7,6},{8,9},{9,8},{10,11... | collective-permute-start | bytes 98312 | tf_op jit(solution)/shard_map/ppermute | solution.py:24
  93.9 5.8 %collective-permute-start.29 = (bf16[128,128]{1,0:T(8,128)(2,1)S(1)}, bf16[128,128]{1,0:T(8,128)(2,1)S(1)}, u32[]{:S(2)}, u32[]{:S(2)}) collective-permute-start(bf16[128,128]{1,0:T(8,128)(2,1)S(1)} %get-tuple-element.46), channel_id=1, source_target_pairs={{1,2},{2,1},{3,4},{4,3},{5,6},{6,5},{7,8},{8,7},{9,10},{10,9},{11,... | collective-permute-start | bytes 98312 | tf_op jit(solution)/shard_map/ppermute | solution.py:24
  101.0 14.8 %collective-permute-start.30 = (bf16[128,128]{1,0:T(8,128)(2,1)}, bf16[128,128]{1,0:T(8,128)(2,1)}, u32[]{:S(2)}, u32[]{:S(2)}) collective-permute-start(bf16[128,128]{1,0:T(8,128)(2,1)} %get-tuple-element.43), channel_id=1, source_target_pairs={{0,128},{128,0},{256,384},{384,256},{1,129},{129,1},{257,385},{385... | collective-permute-start | bytes 98312 | tf_op jit(solution)/shard_map/ppermute | solution.py:24
  104.7 16.7 %collective-permute-start.31 = (bf16[128,128]{1,0:T(8,128)(2,1)}, bf16[128,128]{1,0:T(8,128)(2,1)}, u32[]{:S(2)}, u32[]{:S(2)}) collective-permute-start(bf16[128,128]{1,0:T(8,128)(2,1)} %get-tuple-element.44), channel_id=1, source_target_pairs={{128,256},{256,128},{129,257},{257,129},{130,258},{258,130},{131,2... | collective-permute-start | bytes 98312 | tf_op jit(solution)/shard_map/ppermute | solution.py:24
  108.7 14.4 %collective-permute-start.32 = (bf16[128,128]{1,0:T(8,128)(2,1)}, bf16[128,128]{1,0:T(8,128)(2,1)S(1)}, u32[]{:S(2)}, u32[]{:S(2)}) collective-permute-start(bf16[128,128]{1,0:T(8,128)(2,1)} %get-tuple-element.41), channel_id=1, source_target_pairs={{0,32},{32,0},{64,96},{96,64},{1,33},{33,1},{65,97},{97,65},{2,34}... | collective-permute-start | bytes 98312 | tf_op jit(solution)/shard_map/ppermute | solution.py:24
  113.2 9.8 %collective-permute-start.33 = (bf16[128,128]{1,0:T(8,128)(2,1)}, bf16[128,128]{1,0:T(8,128)(2,1)S(1)}, u32[]{:S(2)}, u32[]{:S(2)}) collective-permute-start(bf16[128,128]{1,0:T(8,128)(2,1)} %get-tuple-element.42), channel_id=1, source_target_pairs={{32,64},{64,32},{33,65},{65,33},{34,66},{66,34},{35,67},{67,35},{3... | collective-permute-start | bytes 98312 | tf_op jit(solution)/shard_map/ppermute | solution.py:24
  113.9 9.2 %collective-permute-start.34 = (bf16[128,128]{1,0:T(8,128)(2,1)}, bf16[128,128]{1,0:T(8,128)(2,1)S(1)}, u32[]{:S(2)}, u32[]{:S(2)}) collective-permute-start(bf16[128,128]{1,0:T(8,128)(2,1)} %get-tuple-element.45), channel_id=1, source_target_pairs={{0,1},{1,0},{2,3},{3,2},{4,5},{5,4},{6,7},{7,6},{8,9},{9,8},{10,11... | collective-permute-start | bytes 98312 | tf_op jit(solution)/shard_map/ppermute | solution.py:24
  115.9 7.3 %collective-permute-start.35 = (bf16[128,128]{1,0:T(8,128)(2,1)}, bf16[128,128]{1,0:T(8,128)(2,1)S(1)}, u32[]{:S(2)}, u32[]{:S(2)}) collective-permute-start(bf16[128,128]{1,0:T(8,128)(2,1)} %get-tuple-element.40), channel_id=1, source_target_pairs={{1,2},{2,1},{3,4},{4,3},{5,6},{6,5},{7,8},{8,7},{9,10},{10,9},{11,... | collective-permute-start | bytes 98312 | tf_op jit(solution)/shard_map/ppermute | solution.py:24
  (20 other events, 266.3 us)
